TPU v7x, 32 devices: a whole 2x2x4 slice. The times are simulated.
32 devices in a mesh: ka: 4 (over y, x), hist: 8 (over z, core).
Axes of the slice: x: 2, y: 2, z: 4, core: 2. Of those that a mesh axis runs over, the one named last changes fastest.
Arguments:
- step_index: int32 [1], replicated, may hold values from 9 to 32
- band_energy: float32 [32, 3, 512], P('hist', None, 'ka'), may hold values from -1 to 3
- kernel_row: bfloat16 [32, 2, 3, 3, 512], P('hist', None, None, None, 'ka'), may hold values from -0.5 to 0.5
- lattice_history: bfloat16 [32, 2, 3, 3, 32, 512], P('hist', None, None, None, None, 'ka'), may hold values from -6 to 6, as said below
- diagonal_inverse: float32 [2, 3, 3, 512], P(None, None, None, 'ka'), may hold values from -3 to 3
- multiplicity: int32 [512], P('ka'), may hold values from 1 to 32, as said below
- state_energy: float32 [64], replicated, may hold values from -3 to 3
- connection: int32 [64, 6], replicated, may hold values from 0 to 63, as said below
- predicted_row: float32 [2, 64, 32], P(None, None, 'hist'), may hold values from -6 to 6
- pseudo_history: bfloat16 [32, 2, 64, 32], P('hist'), may hold values from -6 to 6, as said below
Outputs:
- lattice_row: bfloat16 [32, 2, 3, 3, 512], P('hist', None, None, None, 'ka')
- local_row: float32 [2, 3, 3, 32], P(None, None, None, 'hist')
- pseudo_row: float32 [2, 64, 32], P(None, None, 'hist')
Inputs may be any that keep to these rules, and one draw needn't show every extreme that they name: `lattice_history`: the stored lattice propagators vanish where the column time j exceeds the row time m. `pseudo_history`: the stored pseudo-particle propagators vanish where the column time j exceeds the row time m. `multiplicity`: powers of two. For each flavour f, s -> connection[s, f] is an involution without fixed points; two states that flavour f links differ in that flavour's occupation, under a numbering of the states drawn from the seed.
All inputs are finite; a program needn't handle non-finite values.
Results may differ from a plain program's by a relative error of at most 0.012.
Values may be sent and summed in bfloat16 or wider, within the bound.
A program may use at most 64 MiB of HBM per device.

v0:
```python
import functools

import jax
import jax.numpy as jnp
from jax import lax
from jax.experimental import pallas as pl
from jax.experimental.pallas import tpu as pltpu
from jax.sharding import PartitionSpec as P

time_step = 0.05
coupling = 0.02
tile_rows = 16
highest = lax.Precision.HIGHEST


def weighted_sums(mult, values):
    upper = values.astype(jnp.bfloat16)
    lower = (values - upper.astype(jnp.float32)).astype(jnp.bfloat16)
    return dot_rows(mult, upper) + dot_rows(mult, lower)


def dot_rows(left, right, precision=None):
    return lax.dot_general(
        left,
        right,
        (((1,), (1,)), ((), ())),
        precision=precision,
        preferred_element_type=jnp.float32,
    )


def kernel(
    n_hist,
    n_ka,
    step_ref,
    band_any,
    krow_any,
    hist_any,
    dinv_any,
    mult_any,
    energy_any,
    conn_any,
    pred_any,
    pseudo_any,
    total_out,
    local_out,
    pseudo_out,
    band_ref,
    krow_ref,
    hist_ref,
    dinv_ref,
    mult_ref,
    energy_ref,
    conn_ref,
    pred_ref,
    pseudo_ref,
    kw,
    suffix,
    stage,
    esend,
    erecv,
    lsend,
    lrecv,
    psend,
    precv,
    drep,
    frep,
    total,
    ksend,
    krecv,
    turned,
    qsend,
    qrecv,
    load_sem,
    esend_sem,
    erecv_sem,
    lsend_sem,
    lrecv_sem,
    psend_sem,
    precv_sem,
    ksend_sem,
    krecv_sem,
    qsend_sem,
    qrecv_sem,
):
    orb, block, lanes = band_ref.shape
    times = hist_ref.shape[4]
    states = energy_ref.shape[1]
    pairs = 2 * orb * orb
    rows = pairs * block
    per_tile = tile_rows // block
    me = lax.axis_index("hist")
    my_ka = lax.axis_index("ka")

    barrier = pltpu.get_barrier_semaphore()

    def greet(hop, carry):
        pl.semaphore_signal(
            barrier, inc=1, device_id={"hist": lax.rem(me + hop, n_hist)},
            device_id_type=pl.DeviceIdType.MESH,
        )
        return carry

    lax.fori_loop(1, n_hist, greet, 0)
    for hop in range(1, n_ka):
        pl.semaphore_signal(
            barrier, inc=1, device_id={"ka": lax.rem(my_ka + hop, n_ka)},
            device_id_type=pl.DeviceIdType.MESH,
        )

    sources = (
        krow_any, band_any, mult_any, hist_any, dinv_any, energy_any, conn_any, pred_any, pseudo_any
    )
    targets = (
        krow_ref, band_ref, mult_ref, hist_ref, dinv_ref, energy_ref, conn_ref, pred_ref, pseudo_ref
    )
    loads = [
        pltpu.make_async_copy(source, target, load_sem.at[i])
        for i, (source, target) in enumerate(zip(sources, targets))
    ]
    for load in loads:
        load.start()

    current = step_ref[0]
    first = me * block
    before = [jnp.where(first + m < current, 1.0, 0.0) for m in range(block)]
    weight = [
        jnp.where(first + m == 0, 0.5, 1.0) * before[m] for m in range(block)
    ]

    for load in loads[:3]:
        load.wait()
    for m in range(block):
        kw[m] = krow_ref[m].astype(jnp.float32) * weight[m]

    esend[...] = jnp.zeros(esend.shape, jnp.float32)
    for c in range(orb):
        run = jnp.zeros((1, lanes), jnp.float32)
        for m in reversed(range(block)):
            run = run + band_ref[c, m : m + 1, :] * before[m]
            suffix[c * block + m : c * block + m + 1, :] = run
        esend[c : c + 1, :] = run
    mult = jnp.broadcast_to(mult_ref[...].astype(jnp.float32), (8, lanes)).astype(jnp.bfloat16)

    pl.semaphore_wait(barrier, n_hist - 1 + n_ka - 1)

    def hist_copy(src, dst, send_sem, recv_sem, source, target):
        return pltpu.make_async_remote_copy(
            src_ref=src,
            dst_ref=dst.at[source],
            send_sem=send_sem.at[target],
            recv_sem=recv_sem.at[source],
            device_id={"hist": target},
            device_id_type=pl.DeviceIdType.MESH,
        )

    def energy_copy(source, target):
        return hist_copy(esend, erecv, esend_sem, erecv_sem, source, target)

    def sum_copy(source, target):
        return hist_copy(lsend.at[target], lrecv, lsend_sem, lrecv_sem, source, target)

    def part_copy(source, target):
        return hist_copy(psend.at[target], precv, psend_sem, precv_sem, source, target)

    def pseudo_copy(source, target):
        return hist_copy(qsend.at[target], qrecv, qsend_sem, qrecv_sem, source, target)

    def give_energy(target, carry):
        energy_copy(me, target).start()
        return carry

    lax.fori_loop(0, me, give_energy, 0)
    for load in loads[3:]:
        load.wait()

    def one_tile(tile, carry):
        at = pl.ds(pl.multiple_of(tile * tile_rows, tile_rows), tile_rows)
        zero = jnp.zeros((tile_rows, lanes), jnp.float32)
        real = [[zero] * orb for _ in range(orb)]
        imag = [[zero] * orb for _ in range(orb)]
        for m in range(block):
            for b in range(orb):
                k_re = [kw[m, a, b, 0:1, :] for a in range(orb)]
                k_im = [kw[m, a, b, 1:2, :] for a in range(orb)]
                for c in range(orb):
                    h_re = hist_ref[m, 0, b, c, at, :].astype(jnp.float32)
                    h_im = hist_ref[m, 1, b, c, at, :].astype(jnp.float32)
                    for a in range(orb):
                        real[a][c] += k_re[a] * h_re - k_im[a] * h_im
                        imag[a][c] += k_re[a] * h_im + k_im[a] * h_re
        for a in range(orb):
            for c in range(orb):
                out_re, out_im = zero, zero
                for b in range(orb):
                    d_re = dinv_ref[a, b, 0:1, :]
                    d_im = dinv_ref[a, b, 1:2, :]
                    out_re += d_re * real[b][c] - d_im * imag[b][c]
                    out_im += d_re * imag[b][c] + d_im * real[b][c]
                for s, value in enumerate((out_re, out_im)):
                    row = ((s * orb + a) * orb + c) * block
                    for d in range(per_tile):
                        stage[d, row : row + block, :] = value[d * block : (d + 1) * block]
        sums = weighted_sums(mult, stage[...].reshape(per_tile * rows, lanes))
        for d in range(per_tile):
            target = tile * per_tile + d
            lsend[target, :, :rows] = sums[:1, d * rows : (d + 1) * rows]

            @pl.when(target < me)
            def _():
                sum_copy(me, target).start()

        for d in range(per_tile):
            psend[tile * per_tile + d] = stage[d].astype(jnp.bfloat16)
        return carry

    lax.fori_loop(0, first // tile_rows + 1, one_tile, 0)

    def give_part(target, carry):
        part_copy(me, target).start()
        return carry

    lax.fori_loop(0, me, give_part, 0)

    for s in range(2):
        for a in range(orb):
            for c in range(orb):
                row = ((s * orb + a) * orb + c) * block
                drep[row : row + block, :] = jnp.broadcast_to(
                    dinv_ref[a, c, s : s + 1, :], (block, lanes)
                )
    total[rows:, :] = jnp.ones((lanes - rows, lanes), jnp.float32)
    for m in range(block):
        h_re = pseudo_ref[m, 0].astype(jnp.float32)
        h_im = pseudo_ref[m, 1].astype(jnp.float32)
        turned[m, 0] = jnp.concatenate([h_re, h_im], axis=1)
        turned[m, 1] = jnp.concatenate([-h_im, h_re], axis=1)

    row_of = lax.broadcasted_iota(jnp.int32, (block, 2 * states), 0)
    lane_of = lax.broadcasted_iota(jnp.int32, (block, 2 * states), 1)
    row_time = first + row_of
    row_weight = jnp.where(row_time == 0, 0.5, 1.0) * jnp.where(row_time < current, 1.0, 0.0)
    conn = jnp.concatenate([conn_ref[...], conn_ref[...]], axis=1)
    reach = lax.broadcasted_iota(jnp.int32, (states, 2 * states), 0)
    reached = []
    for a in range(orb):
        hit = jnp.where(conn[2 * a : 2 * a + 1] == reach, 1.0, 0.0) + jnp.where(
            conn[2 * a + 1 : 2 * a + 2] == reach, 1.0, 0.0
        )
        reached.append(
            [
                jnp.dot(pred_ref[p], hit, precision=highest, preferred_element_type=jnp.float32)
                * row_weight
                * coupling
                for p in range(2)
            ]
        )
    energies = jnp.concatenate([energy_ref[...], energy_ref[...]], axis=1)
    spins = energies * time_step * (current - row_time).astype(jnp.float32)
    free_pseudo = jnp.where(lane_of < states, -jnp.sin(spins), -jnp.cos(spins))
    free_pseudo = free_pseudo * jnp.where(row_time <= current, 1.0, 0.0)

    def take_energy(source, later):
        energy_copy(source, me).wait_recv()
        return later + erecv[source]

    later = lax.fori_loop(
        me + 1, n_hist, take_energy, jnp.zeros(esend.shape, jnp.float32)
    )
    for c in range(orb):
        for j in range(block):
            frep[c * block + j : c * block + j + 1, :] = (
                later[c : c + 1] + suffix[c * block + j : c * block + j + 1, :]
            )
    size = orb * block
    angle = time_step * frep[:size, :]
    when = first + lax.rem(lax.broadcasted_iota(jnp.int32, (size, lanes), 0), block)
    inside = jnp.where(when <= current, 1.0, 0.0)
    free_re = -jnp.sin(angle) * inside
    free_im = -jnp.cos(angle) * inside
    for a in range(orb):
        frep[a * size : (a + 1) * size, :] = free_re
        frep[(orb + a) * size : (orb + a + 1) * size, :] = free_im
    half = rows // 2
    f_re, f_im = frep[:half, :], frep[half:, :]
    d_re, d_im = drep[:half, :], drep[half:, :]
    total[:half, :] = d_re * f_re - d_im * f_im
    total[half:rows, :] = d_re * f_im + d_im * f_re

    free_sums = weighted_sums(mult, total[...])[:1]

    def take_sum(source, value):
        sum_copy(source, me).wait_recv()
        return value + lrecv[source][:, :rows]

    own_sums = lsend[me][:, :rows] + free_sums[:, :rows]
    ksend[...] = free_sums
    ksend[:, :rows] = lax.fori_loop(me + 1, n_hist, take_sum, own_sums)

    def local_copy(source, target):
        return pltpu.make_async_remote_copy(
            src_ref=ksend,
            dst_ref=krecv.at[source],
            send_sem=ksend_sem.at[target],
            recv_sem=krecv_sem.at[source],
            device_id={"ka": target},
            device_id_type=pl.DeviceIdType.MESH,
        )

    for hop in range(1, n_ka):
        local_copy(my_ka, lax.rem(my_ka + hop, n_ka)).start()
    local = ksend[...]
    for hop in range(1, n_ka):
        source = lax.rem(my_ka + hop, n_ka)
        local_copy(source, my_ka).wait_recv()
        local = local + krecv[source]
    local = jnp.broadcast_to(local / local[:, rows : rows + 1], (8, lanes))
    local_out[...] = local

    lane8 = lax.broadcasted_iota(jnp.int32, local.shape, 1)
    row8 = lax.broadcasted_iota(jnp.int32, local.shape, 0)

    def diagonal(s, a):
        lane = ((s * orb + a) * orb + a) * block + row8
        picked = jnp.where((lane8 == lane) & (row8 < block), local, 0.0)
        return jnp.sum(picked, axis=1, keepdims=True)[:block]

    self_re = jnp.zeros((block, 2 * states), jnp.float32)
    self_im = self_re
    for a in range(orb):
        h_re, h_im = diagonal(0, a), diagonal(1, a)
        r_re, r_im = reached[a]
        self_re += h_re * r_re - h_im * r_im
        self_im += h_re * r_im + h_im * r_re
    part = jnp.zeros((times, 2 * states), jnp.float32)
    for m in range(block):
        part += self_re[m : m + 1] * turned[m, 0] + self_im[m : m + 1] * turned[m, 1]
    for q in range(n_hist):
        qsend[q] = part[q * block : (q + 1) * block]

    def give_pseudo(target, carry):
        pseudo_copy(me, target).start()
        return carry

    lax.fori_loop(0, me, give_pseudo, 0)

    def take_part(source, value):
        part_copy(source, me).wait_recv()
        return value + precv[source].astype(jnp.float32)

    fresh = total[:rows, :] + psend[me].astype(jnp.float32)
    total_out[...] = lax.fori_loop(me + 1, n_hist, take_part, fresh)

    def take_pseudo(source, value):
        pseudo_copy(source, me).wait_recv()
        return value + qrecv[source]

    pseudo_out[...] = lax.fori_loop(me + 1, n_hist, take_pseudo, free_pseudo + qsend[me])

    def settle(target, carry):
        energy_copy(me, target).wait_send()
        sum_copy(me, target).wait_send()
        part_copy(me, target).wait_send()
        pseudo_copy(me, target).wait_send()
        return carry

    lax.fori_loop(0, me, settle, 0)
    for hop in range(1, n_ka):
        local_copy(my_ka, lax.rem(my_ka + hop, n_ka)).wait_send()


def lay_out(total_ref, local_ref, pseudo_ref, lattice_out, local_out, pseudo_out):
    block, orb = lattice_out.shape[:2]
    states = pseudo_out.shape[2]
    half = total_ref.shape[0] // 2
    for a in range(orb):
        for c in range(orb):
            row = (a * orb + c) * block
            for j in range(block):
                pair = total_ref[pl.ds(row + j, 2, stride=half), :]
                lattice_out[j, a, c] = pair.astype(jnp.bfloat16)
            for s in range(2):
                at = s * half + row
                local_out[a, c, s : s + 1, :] = local_ref[0:1, at : at + block]
    for p in range(2):
        pseudo_out[p] = pseudo_ref[:, p * states : (p + 1) * states]


def per_device(
    n_hist,
    n_ka,
    step_index,
    band_energy,
    kernel_row,
    lattice_history,
    diagonal_inverse,
    multiplicity,
    state_energy,
    connection,
    predicted_row,
    pseudo_history,
):
    block, orb, lanes = band_energy.shape
    times = lattice_history.shape[4]
    states = state_energy.shape[0]
    pairs = 2 * orb * orb
    rows = pairs * block
    per_tile = tile_rows // block
    vmem = pl.BlockSpec(memory_space=pltpu.VMEM)
    f32, bf16 = jnp.float32, jnp.bfloat16
    dma = pltpu.SemaphoreType.DMA
    operands = (
        jnp.transpose(band_energy, (1, 0, 2)),
        jnp.transpose(kernel_row, (0, 2, 3, 1, 4)),
        lattice_history,
        jnp.transpose(diagonal_inverse, (1, 2, 0, 3)),
        multiplicity[None],
        state_energy[None],
        jnp.transpose(connection),
        jnp.transpose(predicted_row, (0, 2, 1)),
        jnp.transpose(pseudo_history, (0, 1, 3, 2)),
    )
    results = pl.pallas_call(
        functools.partial(kernel, n_hist, n_ka),
        out_shape=(
            jax.ShapeDtypeStruct((rows, lanes), f32),
            jax.ShapeDtypeStruct((8, lanes), f32),
            jax.ShapeDtypeStruct((block, 2 * states), f32),
        ),
        in_specs=[pl.BlockSpec(memory_space=pltpu.SMEM)]
        + [pl.BlockSpec(memory_space=pl.ANY)] * len(operands),
        out_specs=(vmem, vmem, vmem),
        scratch_shapes=[
            *[pltpu.VMEM(array.shape, array.dtype) for array in operands],
            pltpu.VMEM((block, orb, orb, 2, lanes), f32),
            pltpu.VMEM((orb * block, lanes), f32),
            pltpu.VMEM((per_tile, rows, lanes), f32),
            pltpu.VMEM((8, lanes), f32),
            pltpu.VMEM((n_hist, 8, lanes), f32),
            pltpu.VMEM((n_hist, 1, lanes), f32),
            pltpu.VMEM((n_hist, 1, lanes), f32),
            pltpu.VMEM((n_hist, rows, lanes), bf16),
            pltpu.VMEM((n_hist, rows, lanes), bf16),
            pltpu.VMEM((rows, lanes), f32),
            pltpu.VMEM((rows, lanes), f32),
            pltpu.VMEM((lanes, lanes), f32),
            pltpu.VMEM((1, lanes), f32),
            pltpu.VMEM((n_ka, 1, lanes), f32),
            pltpu.VMEM((block, 2, times, 2 * states), f32),
            pltpu.VMEM((n_hist, block, 2 * states), f32),
            pltpu.VMEM((n_hist, block, 2 * states), f32),
            dma((len(operands),)),
            dma((n_hist,)),
            dma((n_hist,)),
            dma((n_hist,)),
            dma((n_hist,)),
            dma((n_hist,)),
            dma((n_hist,)),
            dma((n_ka,)),
            dma((n_ka,)),
            dma((n_hist,)),
            dma((n_hist,)),
        ],
        compiler_params=pltpu.CompilerParams(collective_id=0, has_side_effects=True),
    )(
        step_index,
        *operands,
    )
    lattice, local, pseudo = pl.pallas_call(
        lay_out,
        out_shape=(
            jax.ShapeDtypeStruct((block, orb, orb, 2, lanes), bf16),
            jax.ShapeDtypeStruct((orb, orb, 2, block), f32),
            jax.ShapeDtypeStruct((2, block, states), f32),
        ),
        in_specs=[vmem] * 3,
        out_specs=(vmem, vmem, vmem),
    )(*results)
    return (
        jnp.transpose(lattice, (0, 3, 1, 2, 4)),
        jnp.transpose(local, (2, 0, 1, 3)),
        jnp.transpose(pseudo, (0, 2, 1)),
    )


def solution(mesh):
    in_specs = (
        P(),
        P("hist", None, "ka"),
        P("hist", None, None, None, "ka"),
        P("hist", None, None, None, None, "ka"),
        P(None, None, None, "ka"),
        P("ka"),
        P(),
        P(),
        P(None, None, "hist"),
        P("hist", None, None, None),
    )
    out_specs = (
        P("hist", None, None, None, "ka"),
        P(None, None, None, "hist"),
        P(None, None, "hist"),
    )
    return jax.shard_map(
        functools.partial(per_device, mesh.shape["hist"], mesh.shape["ka"]),
        mesh=mesh,
        in_specs=in_specs,
        out_specs=out_specs,
        check_vma=False,
    )
```

profile of v0, /device:TPU:0, one launch (start us, length us, event | category | flops | bytes accessed | tf_op | source)
XLA Modules:
  0.0 19.4 jit_solution(5205755170521817173)
XLA Ops:
  1.3 16.6 %shard_map.121 = (f32[72,128]{1,0:T(8,128)}, f32[8,128]{1,0:T(8,128)}, f32[4,128]{1,0:T(4,128)}) custom-call(s32[1]{0:T(128)S(6)} %copy.13.step_ref, f32[3,4,128]{2,1,0:T(4,128)} %bitcast.14, bf16[4,3,3,2,128]{4,3,2,1,0:T(2,128)(2,1)} %bitcast.12, bf16[4,2,3,3,32,128]{5,4,3,2,1,0:T(8,128)(2,1)} %hist_any.1, f32[3,3,2,128]{3,2,1,0:T(2,128)} %bitcast.13, ...), custom_call_target="tpu_custom_call" | custom-call | tf_op jit(solution)/shard_map/pallas_call | solution.py:423
  17.9 1.5 %shard_map.122 = (bf16[4,3,3,2,128]{4,3,2,1,0:T(2,128)(2,1)}, f32[3,3,2,4]{3,2,1,0:T(2,128)}, f32[2,4,64]{2,1,0:T(4,128)}) custom-call(f32[72,128]{1,0:T(8,128)} %get-tuple-element.9.total_ref, f32[8,128]{1,0:T(8,128)} %get-tuple-element.10.local_ref, f32[4,128]{1,0:T(4,128)} %get-tuple-element.11.pseudo_ref), custom_call_target="tpu_custom_call" | custom-call | tf_op jit(solution)/shard_map/pallas_call | solution.py:469
where the time goes:
time: 19.6 us; the launch traced here: 19.4 us
  Pallas kernels  18.1 us (92%)
  between operations  1.29 us (7%)
    pallas_call x1, Pallas kernels, per_device(): pl.pallas_call(functools.partial(kernel, n_hist, n_ka), out_shape=(jax.Sh...  16.6 us
    pallas_call x1, Pallas kernels, per_device(): pl.pallas_call(lay_out, out_shape=(jax.ShapeDtypeStruct((block, orb, orb,...  1.46 us

commit v1 on v0

--- a/solution.py
+++ b/solution.py
@@ -10,6 +10,7 @@
 time_step = 0.05
 coupling = 0.02
 tile_rows = 16
+layout_bytes = 4 * 1024 * 1024
 highest = lax.Precision.HIGHEST
 
 
@@ -423,9 +424,9 @@
     results = pl.pallas_call(
         functools.partial(kernel, n_hist, n_ka),
         out_shape=(
-            jax.ShapeDtypeStruct((rows, lanes), f32),
-            jax.ShapeDtypeStruct((8, lanes), f32),
-            jax.ShapeDtypeStruct((block, 2 * states), f32),
+            pltpu.VMEM((rows, lanes), f32),
+            pltpu.VMEM((8, lanes), f32),
+            pltpu.VMEM((block, 2 * states), f32),
         ),
         in_specs=[pl.BlockSpec(memory_space=pltpu.SMEM)]
         + [pl.BlockSpec(memory_space=pl.ANY)] * len(operands),
@@ -475,6 +476,7 @@
         ),
         in_specs=[vmem] * 3,
         out_specs=(vmem, vmem, vmem),
+        compiler_params=pltpu.CompilerParams(vmem_limit_bytes=layout_bytes),
     )(*results)
     return (
         jnp.transpose(lattice, (0, 3, 1, 2, 4)),

time: 19.6 us -> 18.1 us (0.923)
  Pallas kernels: 18.1 us -> 16.7 us
    pallas_call x1, Pallas kernels: 1.46 us -> 0.69 us  [per_device(): pl.pallas_call(lay_out, out_shape=(jax.ShapeDtypeStruct((block, orb, orb,...]
    pallas_call x1, Pallas kernels: 16.6 us -> 16 us  [per_device(): pl.pallas_call(functools.partial(kernel, n_hist, n_ka), out_shape=(pltpu....]
where the time goes in v1:
time: 18.1 us; the launch traced here: 18 us
  Pallas kernels  16.7 us (92%)
  between operations  1.29 us (7%)
    pallas_call x1, Pallas kernels, per_device(): pl.pallas_call(functools.partial(kernel, n_hist, n_ka), out_shape=(pltpu....  16 us
    pallas_call x1, Pallas kernels, per_device(): pl.pallas_call(lay_out, out_shape=(jax.ShapeDtypeStruct((block, orb, orb,...  0.69 us

profile of v1, /device:TPU:0, one launch (start us, length us, event | category | flops | bytes accessed | tf_op | source)
XLA Modules:
  0.0 18.0 jit_solution(5547840163102868803)
XLA Ops:
  1.3 16.0 %shard_map.121 = (f32[72,128]{1,0:T(8,128)S(1)}, f32[8,128]{1,0:T(8,128)S(1)}, f32[4,128]{1,0:T(4,128)S(1)}) custom-call(s32[1]{0:T(128)S(6)} %copy.13.step_ref, f32[3,4,128]{2,1,0:T(4,128)} %bitcast.14, bf16[4,3,3,2,128]{4,3,2,1,0:T(2,128)(2,1)} %bitcast.12, bf16[4,2,3,3,32,128]{5,4,3,2,1,0:T(8,128)(2,1)} %hist_any.1, f32[3,3,2,128]{3,2,1,0:T(2,128)} %bitcast.13, ...), custom_call_target="tpu_custom_call" | custom-call | tf_op jit(solution)/shard_map/pallas_call | solution.py:424
  17.3 0.7 %shard_map.122 = (bf16[4,3,3,2,128]{4,3,2,1,0:T(2,128)(2,1)}, f32[3,3,2,4]{3,2,1,0:T(2,128)}, f32[2,4,64]{2,1,0:T(4,128)}) custom-call(f32[72,128]{1,0:T(8,128)S(1)} %get-tuple-element.9.total_ref, f32[8,128]{1,0:T(8,128)S(1)} %get-tuple-element.10.local_ref, f32[4,128]{1,0:T(4,128)S(1)} %get-tuple-element.11.pseudo_ref), custom_call_target="tpu_custom_call" | custom-call | tf_op jit(solution)/shard_map/pallas_call | solution.py:470

commit v2 on v1

v2 whole, which is shorter than its diff:
```python
import functools

import jax
import jax.numpy as jnp
from jax import lax
from jax.experimental import pallas as pl
from jax.experimental.pallas import tpu as pltpu
from jax.sharding import PartitionSpec as P

time_step = 0.05
coupling = 0.02
tile_rows = 16
group_rows = 8
lane_count = 128
layout_bytes = 4 * 1024 * 1024


def two_parts(values):
    upper = values.astype(jnp.bfloat16).astype(jnp.float32)
    return upper, values - upper


def stacked(values):
    return jnp.concatenate(two_parts(values), axis=0).astype(jnp.bfloat16)


def dot(left, right, contract):
    return lax.dot_general(
        left,
        right,
        (((1,), (contract,)), ((), ())),
        preferred_element_type=jnp.float32,
    )


def folded(values):
    return values[:group_rows] + values[group_rows:]


def kernel(
    n_hist,
    n_ka,
    step_ref,
    band_any,
    krow_any,
    hist_any,
    dinv_any,
    mult_any,
    energy_any,
    conn_any,
    pred_any,
    pseudo_any,
    total_out,
    local_out,
    pseudo_out,
    band_recv,
    krow_ref,
    hist_ref,
    dinv_ref,
    mult_ref,
    energy_ref,
    conn_ref,
    pred_ref,
    pseudo_ref,
    kw,
    d_same,
    d_turn,
    band_all,
    free_all,
    vsend,
    vrecv,
    xsend,
    xrecv,
    psend,
    precv,
    csend,
    crecv,
    hist_p,
    hist_r,
    hits,
    mix,
    stage,
    load_sem,
    esend_sem,
    erecv_sem,
    vsend_sem,
    vrecv_sem,
    psend_sem,
    precv_sem,
    csend_sem,
    crecv_sem,
    xsend_sem,
    xrecv_sem,
):
    _, orb, block, lanes = band_recv.shape
    times = hist_ref.shape[4]
    states = energy_ref.shape[1]
    pairs = 2 * orb * orb
    rows = pairs * block
    per_tile = tile_rows // block
    width = vsend.shape[1]
    cols = orb * times
    f32, bf16 = jnp.float32, jnp.bfloat16
    me = lax.axis_index("hist")
    my_ka = lax.axis_index("ka")
    first = me * block

    barrier = pltpu.get_barrier_semaphore()

    def greet(target, carry):
        pl.semaphore_signal(
            barrier, inc=1, device_id={"hist": target}, device_id_type=pl.DeviceIdType.MESH
        )
        return carry

    lax.fori_loop(me + 1, n_hist, greet, 0)
    for hop in range(1, n_ka):
        pl.semaphore_signal(
            barrier, inc=1, device_id={"ka": lax.rem(my_ka + hop, n_ka)},
            device_id_type=pl.DeviceIdType.MESH,
        )

    sources = (
        krow_any, dinv_any, mult_any, hist_any, band_any, pred_any, pseudo_any, energy_any, conn_any
    )
    targets = (
        krow_ref, dinv_ref, mult_ref, hist_ref, band_recv.at[me], pred_ref, pseudo_ref, energy_ref,
        conn_ref,
    )
    loads = [
        pltpu.make_async_copy(source, target, load_sem.at[i])
        for i, (source, target) in enumerate(zip(sources, targets))
    ]
    for load in loads:
        load.start()

    def hist_copy(src, dst, send_sem, recv_sem, source, target):
        return pltpu.make_async_remote_copy(
            src_ref=src,
            dst_ref=dst.at[source],
            send_sem=send_sem.at[target],
            recv_sem=recv_sem.at[source],
            device_id={"hist": target},
            device_id_type=pl.DeviceIdType.MESH,
        )

    def energy_copy(source, target):
        return hist_copy(band_any, band_recv, esend_sem, erecv_sem, source, target)

    def sum_copy(source, target):
        return hist_copy(vsend, vrecv, vsend_sem, vrecv_sem, source, target)

    def part_copy(source, target):
        return hist_copy(psend.at[target], precv, psend_sem, precv_sem, source, target)

    def column_copy(source, target):
        return hist_copy(csend.at[target], crecv, csend_sem, crecv_sem, source, target)

    def local_copy(source, target):
        return pltpu.make_async_remote_copy(
            src_ref=xsend,
            dst_ref=xrecv.at[source],
            send_sem=xsend_sem.at[target],
            recv_sem=xrecv_sem.at[source],
            device_id={"ka": target},
            device_id_type=pl.DeviceIdType.MESH,
        )

    def give(copy):
        def one(target, carry):
            copy(me, target).start()
            return carry

        lax.fori_loop(0, me, one, 0)

    def take(copy):
        def one(source, carry):
            copy(source, me).wait_recv()
            return carry

        lax.fori_loop(me + 1, n_hist, one, 0)

    current = step_ref[0]
    weight = [
        jnp.where(first + m == 0, 0.5, 1.0) * jnp.where(first + m < current, 1.0, 0.0)
        for m in range(block)
    ]
    d_same[...] = jnp.zeros(d_same.shape, f32)
    d_turn[...] = jnp.zeros(d_turn.shape, f32)
    vsend[...] = jnp.zeros(vsend.shape, f32)

    with jax.named_scope("WBAR"):
        pl.semaphore_wait(barrier, me + n_ka - 1)
    give(energy_copy)

    with jax.named_scope("LOAD"):
        for load in loads[:3]:
            load.wait()
    mult = mult_ref[...].astype(f32)
    for m in range(block):
        kw[m] = krow_ref[m].astype(f32) * weight[m]
    for a in range(orb):
        for c in range(orb):
            d_re = dinv_ref[a, c, 0:1, :] * mult
            d_im = dinv_ref[a, c, 1:2, :] * mult
            d_same[c, a : a + 1, :] = d_re
            d_same[c, orb + a : orb + a + 1, :] = d_im
            d_turn[c, a : a + 1, :] = -d_im
            d_turn[c, orb + a : orb + a + 1, :] = d_re
    same = [d_same[c] for c in range(orb)]
    turn = [d_turn[c] for c in range(orb)]
    with jax.named_scope("LOADH"):
        loads[3].wait()
    left, right = [], []
    for m in range(block):
        for b in range(orb):
            plain = jnp.zeros((group_rows, lanes), f32)
            turned = plain
            for c in range(orb):
                k_re = kw[m, c, b, 0:1, :]
                k_im = kw[m, c, b, 1:2, :]
                plain += same[c] * k_re + turn[c] * k_im
                turned += turn[c] * k_re - same[c] * k_im
            for p, factor in enumerate((plain, turned)):
                left.append(stacked(factor))
                right.append(hist_ref[m, p, b].reshape(cols, lanes))
    with jax.named_scope("VDOT"):
        sums = dot(jnp.concatenate(left, axis=1), jnp.concatenate(right, axis=1), 1)
        vsend[:, :cols] = folded(sums)
    give(sum_copy)

    with jax.named_scope("PC"):
        for load in loads[4:]:
            load.wait()
        half = group_rows * 2
        for m in range(block):
            h_re = pseudo_ref[m, 0].astype(f32)
            h_im = pseudo_ref[m, 1].astype(f32)
            both = jnp.concatenate([h_re, h_im], axis=1)
            for t in range(n_hist):
                hist_p[t * half + m * block : t * half + (m + 1) * block, :] = both[
                    t * block : (t + 1) * block
                ]
        given = jnp.concatenate([pred_ref[0], pred_ref[1]], axis=1)
        tail = jnp.concatenate(
            [*two_parts(given), jnp.zeros((half - 2 * block, lanes), f32)], axis=0
        ).astype(bf16)
        for t in range(n_hist):
            csend[t, :half, :] = hist_p[t * half : (t + 1) * half, :].astype(bf16)
            csend[t, half:, :] = tail
    give(column_copy)

    def one_tile(tile, carry):
        at = pl.ds(pl.multiple_of(tile * tile_rows, tile_rows), tile_rows)
        zero = jnp.zeros((tile_rows, lanes), f32)
        real = [[zero] * orb for _ in range(orb)]
        imag = [[zero] * orb for _ in range(orb)]
        for m in range(block):
            for b in range(orb):
                k_re = [kw[m, a, b, 0:1, :] for a in range(orb)]
                k_im = [kw[m, a, b, 1:2, :] for a in range(orb)]
                for c in range(orb):
                    h_re = hist_ref[m, 0, b, c, at, :].astype(f32)
                    h_im = hist_ref[m, 1, b, c, at, :].astype(f32)
                    for a in range(orb):
                        real[a][c] += k_re[a] * h_re - k_im[a] * h_im
                        imag[a][c] += k_re[a] * h_im + k_im[a] * h_re
        for a in range(orb):
            for c in range(orb):
                out_re, out_im = zero, zero
                for b in range(orb):
                    d_re = dinv_ref[a, b, 0:1, :]
                    d_im = dinv_ref[a, b, 1:2, :]
                    out_re += d_re * real[b][c] - d_im * imag[b][c]
                    out_im += d_re * imag[b][c] + d_im * real[b][c]
                for s, value in enumerate((out_re, out_im)):
                    row = ((s * orb + a) * orb + c) * block
                    for d in range(per_tile):
                        stage[d, row : row + block, :] = value[d * block : (d + 1) * block]
        for d in range(per_tile):
            target = tile * per_tile + d
            psend[target] = stage[d].astype(bf16)

            @pl.when(target < me)
            def _():
                part_copy(me, target).start()

        return carry

    with jax.named_scope("TILES"):
        lax.fori_loop(0, first // tile_rows + 1, one_tile, 0)

    crecv[me] = csend[me]
    row_of = lax.broadcasted_iota(jnp.int32, (times, lanes), 0)
    lane_of = lax.broadcasted_iota(jnp.int32, (group_rows, width), 1)
    group_of = lax.broadcasted_iota(jnp.int32, (group_rows, width), 0)
    conn = jnp.concatenate([conn_ref[...], conn_ref[...]], axis=1)
    reach = lax.broadcasted_iota(jnp.int32, (2 * states, 2 * states), 0)
    for a in range(orb):
        for p in range(2):
            at = (2 * a + p) * lanes
            hit = jnp.where(conn[2 * a : 2 * a + 1] + p * states == reach, 1.0, 0.0) + jnp.where(
                conn[2 * a + 1 : 2 * a + 2] + p * states == reach, 1.0, 0.0
            )
            hits[:, at : at + 2 * states] = hit.astype(bf16)
    mix[cols:width, :] = jnp.zeros((width - cols, mix.shape[1]), bf16)
    mix[width + cols :, :] = jnp.zeros((width - cols, mix.shape[1]), bf16)
    line = lax.broadcasted_iota(jnp.int32, (block, 2 * states), 0) + first
    lane = lax.broadcasted_iota(jnp.int32, (block, 2 * states), 1)
    energies = jnp.concatenate([energy_ref[...], energy_ref[...]], axis=1)
    spins = energies * time_step * (current - line).astype(f32)
    free_pseudo = jnp.where(lane < states, -jnp.sin(spins), -jnp.cos(spins))
    free_pseudo = free_pseudo * jnp.where(line <= current, 1.0, 0.0)
    count = jnp.sum(mult, axis=1, keepdims=True)
    step_row = lax.broadcasted_iota(jnp.int32, (times, times), 0)
    step_col = lax.broadcasted_iota(jnp.int32, (times, times), 1)
    later = jnp.where((step_col >= step_row) & (step_col < current), 1.0, 0.0).astype(bf16)
    inside = (row_of <= current) & (row_of >= first)

    with jax.named_scope("TAKEE"):
        take(energy_copy)
    with jax.named_scope("FREE"):
        for t in range(n_hist):
            for c in range(orb):
                band_all[c, t * block : (t + 1) * block, :] = band_recv[t, c]
        angle = jnp.zeros((times, orb * lanes), f32)
        rest = jnp.concatenate(
            [jnp.where(row_of >= first, band_all[c], 0.0) for c in range(orb)], axis=1
        )
        for _ in range(3):
            piece = rest.astype(bf16)
            angle += dot(later, piece, 0)
            rest = rest - piece.astype(f32)
        angle = angle * time_step
        pieces = []
        for c in range(orb):
            part = angle[:, c * lanes : (c + 1) * lanes]
            free_re = jnp.where(inside, -jnp.sin(part), 0.0)
            free_im = jnp.where(inside, -jnp.cos(part), 0.0)
            free_all[0, c] = free_re
            free_all[1, c] = free_im
            two_re, two_im = two_parts(free_re), two_parts(free_im)
            right = jnp.concatenate([two_re[0], two_im[0], two_re[1], two_im[1]], axis=1)
            left = jnp.concatenate([stacked(same[c]), stacked(turn[c])] * 2, axis=1)
            pieces.append(folded(dot(left, right.astype(bf16), 1)))
        pieces.append(jnp.zeros((group_rows, width - cols), f32))
        own = jnp.concatenate(pieces, axis=1) + vsend[...]
        own = jnp.where(lane_of == cols, count, own)

    def take_sum(source, value):
        sum_copy(source, me).wait_recv()
        return value + vrecv[source]

    with jax.named_scope("TAKEV"):
        xsend[...] = lax.fori_loop(me + 1, n_hist, take_sum, own)
    for hop in range(1, n_ka):
        local_copy(my_ka, lax.rem(my_ka + hop, n_ka)).start()

    with jax.named_scope("TOTAL"):
        at = pl.ds(pl.multiple_of(first, block), block)
        for c in range(orb):
            f_re = free_all[0, c, at, :]
            f_im = free_all[1, c, at, :]
            for a in range(orb):
                d_re = dinv_ref[a, c, 0:1, :]
                d_im = dinv_ref[a, c, 1:2, :]
                row = (a * orb + c) * block
                total_out[row : row + block, :] = d_re * f_re - d_im * f_im
                row += rows // 2
                total_out[row : row + block, :] = d_re * f_im + d_im * f_re

    with jax.named_scope("TAKEC"):
        take(column_copy)
    with jax.named_scope("MIX"):
        for t in range(n_hist):
            hist_p[t * half : (t + 1) * half, :] = crecv[t, :half, :].astype(f32)
            tail = crecv[t, half:, :].astype(f32)
            for p in range(2):
                at = p * times + t * block
                hist_r[at : at + block, :] = tail[p * block : (p + 1) * block]
        known = jnp.concatenate([row_of >= first] * 2, axis=0)
        given = jnp.where(known, hist_r[...], 0.0).astype(bf16)
        reached = dot(given, hits[...], 0)
        reached = reached[:times] + reached[times:]
        row_weight = jnp.where(row_of == 0, 0.5 * coupling, coupling)
        row_weight = row_weight * jnp.where(row_of < current, 1.0, 0.0)
        sign = jnp.where(
            lax.broadcasted_iota(jnp.int32, (times, lanes), 1) < states, -1.0, 1.0
        )
        r_re = [reached[:, 2 * a * lanes : (2 * a + 1) * lanes] * row_weight for a in range(orb)]
        r_im = [
            reached[:, (2 * a + 1) * lanes : (2 * a + 2) * lanes] * row_weight for a in range(orb)
        ]
        for j in range(block):
            plain = jnp.where(row_of >= first, hist_p[pl.ds(j, times, stride=block), :], 0.0)
            turned = pltpu.roll(plain, states, 1) * sign
            at = slice(j * lanes, (j + 1) * lanes)
            for a in range(orb):
                low, high = a * times, (a + 1) * times
                mix[low:high, at] = (r_re[a] * plain + r_im[a] * turned).astype(bf16)
                mix[width + low : width + high, at] = (
                    r_re[a] * turned - r_im[a] * plain
                ).astype(bf16)

    with jax.named_scope("TAKEX"):
        local = xsend[...]
        for hop in range(1, n_ka):
            source = lax.rem(my_ka + hop, n_ka)
            local_copy(source, my_ka).wait_recv()
            local = local + xrecv[source]
    with jax.named_scope("FINAL"):
        scale = 1.0 / local[:, cols : cols + 1]
        picked = jnp.where(lane_of // times == lax.rem(group_of, orb), local, 0.0)
        picked = jnp.concatenate(
            [jnp.where(group_of < orb, picked, 0.0), jnp.where(group_of < orb, 0.0, picked)], axis=1
        )
        sums = folded(dot(stacked(picked), mix[...], 0))
        sums = jnp.sum(sums, axis=0, keepdims=True)
        for j in range(block):
            pseudo_out[j : j + 1, :] = (
                free_pseudo[j : j + 1] + sums[:, j * lanes : (j + 1) * lanes] * scale[:1]
            )
        local_out[...] = pltpu.roll(local * scale, width - first, 1)

    def take_part(source, value):
        part_copy(source, me).wait_recv()
        return value + precv[source].astype(f32)

    with jax.named_scope("TAKEP"):
        fresh = total_out[...] + psend[me].astype(f32)
        total_out[...] = lax.fori_loop(me + 1, n_hist, take_part, fresh)

    def settle(target, carry):
        energy_copy(me, target).wait_send()
        sum_copy(me, target).wait_send()
        column_copy(me, target).wait_send()
        part_copy(me, target).wait_send()
        return carry

    lax.fori_loop(0, me, settle, 0)
    for hop in range(1, n_ka):
        local_copy(my_ka, lax.rem(my_ka + hop, n_ka)).wait_send()


def lay_out(times, total_ref, local_ref, pseudo_ref, lattice_out, local_out, pseudo_out):
    block, orb = lattice_out.shape[:2]
    states = pseudo_out.shape[2]
    half = total_ref.shape[0] // 2
    for a in range(orb):
        for c in range(orb):
            row = (a * orb + c) * block
            for j in range(block):
                pair = total_ref[pl.ds(row + j, 2, stride=half), :]
                lattice_out[j, a, c] = pair.astype(jnp.bfloat16)
            for s in range(2):
                row = s * orb + a
                local_out[a, c, s : s + 1, :] = local_ref[
                    row : row + 1, c * times : c * times + block
                ]
    for p in range(2):
        pseudo_out[p] = pseudo_ref[:, p * states : (p + 1) * states]


def per_device(
    n_hist,
    n_ka,
    step_index,
    band_energy,
    kernel_row,
    lattice_history,
    diagonal_inverse,
    multiplicity,
    state_energy,
    connection,
    predicted_row,
    pseudo_history,
):
    block, orb, lanes = band_energy.shape
    times = lattice_history.shape[4]
    states = state_energy.shape[0]
    pairs = 2 * orb * orb
    rows = pairs * block
    per_tile = tile_rows // block
    width = -(-(orb * times + 1) // lane_count) * lane_count
    vmem = pl.BlockSpec(memory_space=pltpu.VMEM)
    f32, bf16 = jnp.float32, jnp.bfloat16
    dma = pltpu.SemaphoreType.DMA
    operands = (
        jnp.transpose(band_energy, (1, 0, 2)),
        jnp.transpose(kernel_row, (0, 2, 3, 1, 4)),
        lattice_history,
        jnp.transpose(diagonal_inverse, (1, 2, 0, 3)),
        multiplicity[None],
        state_energy[None],
        jnp.transpose(connection),
        jnp.transpose(predicted_row, (0, 2, 1)),
        jnp.transpose(pseudo_history, (0, 1, 3, 2)),
    )
    results = pl.pallas_call(
        functools.partial(kernel, n_hist, n_ka),
        out_shape=(
            pltpu.VMEM((rows, lanes), f32),
            pltpu.VMEM((group_rows, width), f32),
            pltpu.VMEM((block, 2 * states), f32),
        ),
        in_specs=[pl.BlockSpec(memory_space=pltpu.SMEM)]
        + [pl.BlockSpec(memory_space=pl.ANY)] * len(operands),
        out_specs=(vmem, vmem, vmem),
        scratch_shapes=[
            pltpu.VMEM((n_hist, *operands[0].shape), f32),
            *[pltpu.VMEM(array.shape, array.dtype) for array in operands[1:]],
            pltpu.VMEM((block, orb, orb, 2, lanes), f32),
            pltpu.VMEM((orb, group_rows, lanes), f32),
            pltpu.VMEM((orb, group_rows, lanes), f32),
            pltpu.VMEM((orb, times, lanes), f32),
            pltpu.VMEM((2, orb, times, lanes), f32),
            pltpu.VMEM((group_rows, width), f32),
            pltpu.VMEM((n_hist, group_rows, width), f32),
            pltpu.VMEM((group_rows, width), f32),
            pltpu.VMEM((n_ka, group_rows, width), f32),
            pltpu.VMEM((n_hist, rows, lanes), bf16),
            pltpu.VMEM((n_hist, rows, lanes), bf16),
            pltpu.VMEM((n_hist, 4 * group_rows, lanes), bf16),
            pltpu.VMEM((n_hist, 4 * group_rows, lanes), bf16),
            pltpu.VMEM((times * block, lanes), f32),
            pltpu.VMEM((2 * times, lanes), f32),
            pltpu.VMEM((2 * states, 2 * orb * lanes), bf16),
            pltpu.VMEM((2 * width, 2 * block * states), bf16),
            pltpu.VMEM((per_tile, rows, lanes), f32),
            dma((len(operands),)),
            *[dma((n_hist,)) for _ in range(8)],
            dma((n_ka,)),
            dma((n_ka,)),
        ],
        compiler_params=pltpu.CompilerParams(collective_id=0, has_side_effects=True),
    )(
        step_index,
        *operands,
    )
    lattice, local, pseudo = pl.pallas_call(
        functools.partial(lay_out, times),
        out_shape=(
            jax.ShapeDtypeStruct((block, orb, orb, 2, lanes), bf16),
            jax.ShapeDtypeStruct((orb, orb, 2, block), f32),
            jax.ShapeDtypeStruct((2, block, states), f32),
        ),
        in_specs=[vmem] * 3,
        out_specs=(vmem, vmem, vmem),
        compiler_params=pltpu.CompilerParams(vmem_limit_bytes=layout_bytes),
    )(*results)
    return (
        jnp.transpose(lattice, (0, 3, 1, 2, 4)),
        jnp.transpose(local, (2, 0, 1, 3)),
        jnp.transpose(pseudo, (0, 2, 1)),
    )


def solution(mesh):
    in_specs = (
        P(),
        P("hist", None, "ka"),
        P("hist", None, None, None, "ka"),
        P("hist", None, None, None, None, "ka"),
        P(None, None, None, "ka"),
        P("ka"),
        P(),
        P(),
        P(None, None, "hist"),
        P("hist", None, None, None),
    )
    out_specs = (
        P("hist", None, None, None, "ka"),
        P(None, None, None, "hist"),
        P(None, None, "hist"),
    )
    return jax.shard_map(
        functools.partial(per_device, mesh.shape["hist"], mesh.shape["ka"]),
        mesh=mesh,
        in_specs=in_specs,
        out_specs=out_specs,
        check_vma=False,
    )
```

time: 18.1 us -> 16.5 us (0.912)
  Pallas kernels: 16.7 us -> 15 us
    pallas_call x1, Pallas kernels: 16 us -> 14.4 us  [per_device(): pl.pallas_call(functools.partial(kernel, n_hist, n_ka), out_shape=(pltpu....]
where the time goes in v2:
time: 16.5 us; the launch traced here: 16.3 us
  Pallas kernels  15 us (91%)
  between operations  1.29 us (8%)
    pallas_call x1, Pallas kernels, per_device(): pl.pallas_call(functools.partial(kernel, n_hist, n_ka), out_shape=(pltpu....  14.4 us
    pallas_call x1, Pallas kernels, per_device(): pl.pallas_call(functools.partial(lay_out, times), out_shape=(jax.ShapeDty...  0.68 us

profile of v2, /device:TPU:0, one launch (start us, length us, event | category | flops | bytes accessed | tf_op | source)
XLA Modules:
  0.0 16.3 jit_solution(8270931282621029241)
XLA Ops:
  1.3 14.4 %shard_map.121 = (f32[72,128]{1,0:T(8,128)S(1)}, f32[8,128]{1,0:T(8,128)S(1)}, f32[4,128]{1,0:T(4,128)S(1)}) custom-call(s32[1]{0:T(128)S(6)} %copy.13.step_ref, f32[3,4,128]{2,1,0:T(4,128)} %bitcast.14, bf16[4,3,3,2,128]{4,3,2,1,0:T(2,128)(2,1)} %bitcast.12, bf16[4,2,3,3,32,128]{5,4,3,2,1,0:T(8,128)(2,1)} %hist_any.1, f32[3,3,2,128]{3,2,1,0:T(2,128)} %bitcast.13, ...), custom_call_target="tpu_custom_call" | custom-call | tf_op jit(solution)/shard_map/pallas_call | solution.py:499
  15.6 0.7 %shard_map.122 = (bf16[4,3,3,2,128]{4,3,2,1,0:T(2,128)(2,1)}, f32[3,3,2,4]{3,2,1,0:T(2,128)}, f32[2,4,64]{2,1,0:T(4,128)}) custom-call(f32[72,128]{1,0:T(8,128)S(1)} %get-tuple-element.9.total_ref, f32[8,128]{1,0:T(8,128)S(1)} %get-tuple-element.10.local_ref, f32[4,128]{1,0:T(4,128)S(1)} %get-tuple-element.11.pseudo_ref), custom_call_target="tpu_custom_call" | custom-call | tf_op jit(solution)/shard_map/pallas_call | solution.py:540

commit v3 on v2

--- a/solution.py
+++ b/solution.py
@@ -11,6 +11,7 @@
 coupling = 0.02
 tile_rows = 16
 group_rows = 8
+lead = 2
 lane_count = 128
 layout_bytes = 4 * 1024 * 1024
 
@@ -70,6 +71,7 @@
     vsend,
     vrecv,
     xsend,
+    xfree,
     xrecv,
     psend,
     precv,
@@ -81,16 +83,18 @@
     mix,
     stage,
     load_sem,
-    esend_sem,
-    erecv_sem,
-    vsend_sem,
-    vrecv_sem,
-    psend_sem,
-    precv_sem,
-    csend_sem,
-    crecv_sem,
-    xsend_sem,
-    xrecv_sem,
+    sent_energy,
+    sent_sum,
+    sent_direct,
+    sent_column,
+    sent_part,
+    sent_local,
+    got_energy,
+    got_sum,
+    got_column,
+    got_part,
+    got_local,
+    opened,
 ):
     _, orb, block, lanes = band_recv.shape
     times = hist_ref.shape[4]
@@ -107,78 +111,95 @@
 
     barrier = pltpu.get_barrier_semaphore()
 
+    def signal(sem, hist, ka):
+        pl.semaphore_signal(
+            sem, inc=1, device_id={"hist": hist, "ka": ka}, device_id_type=pl.DeviceIdType.MESH
+        )
+
     def greet(target, carry):
-        pl.semaphore_signal(
-            barrier, inc=1, device_id={"hist": target}, device_id_type=pl.DeviceIdType.MESH
-        )
+        signal(barrier, target, my_ka)
         return carry
 
     lax.fori_loop(me + 1, n_hist, greet, 0)
-    for hop in range(1, n_ka):
-        pl.semaphore_signal(
-            barrier, inc=1, device_id={"ka": lax.rem(my_ka + hop, n_ka)},
+    is_root = (my_ka == 0) & (me < lead)
+
+    @pl.when(is_root)
+    def _():
+        def one(target, carry):
+            for ka in range(1, n_ka):
+                signal(barrier, target, ka)
+            return carry
+
+        lax.fori_loop(me + 1, n_hist, one, 0)
+
+    for ka in range(n_ka):
+
+        @pl.when((me > 0) | (my_ka != ka))
+        def _():
+            signal(barrier, 0, ka)
+
+    def load(source, target, place):
+        copy = pltpu.make_async_copy(source, target, load_sem.at[place])
+        copy.start()
+        return copy
+
+    pairs_in = [(krow_any, krow_ref), (dinv_any, dinv_ref), (mult_any, mult_ref)]
+    pairs_in += [(hist_any.at[m], hist_ref.at[m]) for m in range(block)]
+    pairs_in += [
+        (pred_any, pred_ref),
+        (pseudo_any, pseudo_ref),
+        (energy_any, energy_ref),
+        (conn_any, conn_ref),
+        (band_any, band_recv.at[me]),
+    ]
+    loads = [load(source, target, i) for i, (source, target) in enumerate(pairs_in)]
+    small, large, others = loads[:3], loads[3 : 3 + block], loads[3 + block :]
+
+    def remote(src, dst, send_sem, recv_sem, hist, ka):
+        return pltpu.make_async_remote_copy(
+            src_ref=src,
+            dst_ref=dst,
+            send_sem=send_sem,
+            recv_sem=recv_sem,
+            device_id={"hist": hist, "ka": ka},
             device_id_type=pl.DeviceIdType.MESH,
         )
 
-    sources = (
-        krow_any, dinv_any, mult_any, hist_any, band_any, pred_any, pseudo_any, energy_any, conn_any
-    )
-    targets = (
-        krow_ref, dinv_ref, mult_ref, hist_ref, band_recv.at[me], pred_ref, pseudo_ref, energy_ref,
-        conn_ref,
-    )
-    loads = [
-        pltpu.make_async_copy(source, target, load_sem.at[i])
-        for i, (source, target) in enumerate(zip(sources, targets))
-    ]
-    for load in loads:
-        load.start()
-
-    def hist_copy(src, dst, send_sem, recv_sem, source, target):
-        return pltpu.make_async_remote_copy(
-            src_ref=src,
-            dst_ref=dst.at[source],
-            send_sem=send_sem.at[target],
-            recv_sem=recv_sem.at[source],
-            device_id={"hist": target},
-            device_id_type=pl.DeviceIdType.MESH,
-        )
-
-    def energy_copy(source, target):
-        return hist_copy(band_any, band_recv, esend_sem, erecv_sem, source, target)
-
-    def sum_copy(source, target):
-        return hist_copy(vsend, vrecv, vsend_sem, vrecv_sem, source, target)
-
-    def part_copy(source, target):
-        return hist_copy(psend.at[target], precv, psend_sem, precv_sem, source, target)
-
-    def column_copy(source, target):
-        return hist_copy(csend.at[target], crecv, csend_sem, crecv_sem, source, target)
-
-    def local_copy(source, target):
-        return pltpu.make_async_remote_copy(
-            src_ref=xsend,
-            dst_ref=xrecv.at[source],
-            send_sem=xsend_sem.at[target],
-            recv_sem=xrecv_sem.at[source],
-            device_id={"ka": target},
-            device_id_type=pl.DeviceIdType.MESH,
-        )
-
-    def give(copy):
+    def energy_copy(target):
+        return remote(band_any, band_recv.at[me], sent_energy, got_energy, target, my_ka)
+
+    def sum_copy(target):
+        return remote(vsend, vrecv.at[me, my_ka], sent_sum, got_sum, target, my_ka)
+
+    def direct_copy(target):
+        return remote(vsend, vrecv.at[me, my_ka], sent_direct, got_sum, target, 0)
+
+    def part_copy(target):
+        return remote(psend.at[target], precv.at[me], sent_part, got_part, target, my_ka)
+
+    def column_copy(target):
+        return remote(csend.at[target], crecv.at[me], sent_column, got_column, target, my_ka)
+
+    def local_copy(src, hop):
+        target = lax.rem(my_ka + hop, n_ka)
+        return remote(src, xrecv.at[hop - 1], sent_local, got_local, me, target)
+
+    def give(copy, stop):
         def one(target, carry):
-            copy(me, target).start()
+            copy(target).start()
             return carry
 
-        lax.fori_loop(0, me, one, 0)
-
-    def take(copy):
-        def one(source, carry):
-            copy(source, me).wait_recv()
-            return carry
-
-        lax.fori_loop(me + 1, n_hist, one, 0)
+        lax.fori_loop(0, stop, one, 0)
+
+    def wait_bytes(ref, sem):
+        pltpu.make_async_copy(ref, ref, sem).wait()
+
+    def take(ref, sem):
+        for t in range(n_hist - 1):
+
+            @pl.when(me == t)
+            def _():
+                wait_bytes(ref.at[pl.ds(t + 1, n_hist - 1 - t)], sem)
 
     current = step_ref[0]
     weight = [
@@ -189,13 +210,18 @@
     d_turn[...] = jnp.zeros(d_turn.shape, f32)
     vsend[...] = jnp.zeros(vsend.shape, f32)
 
+    direct = jnp.where(my_ka == 0, 0, jnp.minimum(me, lead))
     with jax.named_scope("WBAR"):
-        pl.semaphore_wait(barrier, me + n_ka - 1)
-    give(energy_copy)
+
+        @pl.when(me > 0)
+        def _():
+            pl.semaphore_wait(barrier, me + direct)
+
+    give(energy_copy, me)
 
     with jax.named_scope("LOAD"):
-        for load in loads[:3]:
-            load.wait()
+        for copy in small:
+            copy.wait()
     mult = mult_ref[...].astype(f32)
     for m in range(block):
         kw[m] = krow_ref[m].astype(f32) * weight[m]
@@ -209,10 +235,9 @@
             d_turn[c, orb + a : orb + a + 1, :] = d_re
     same = [d_same[c] for c in range(orb)]
     turn = [d_turn[c] for c in range(orb)]
-    with jax.named_scope("LOADH"):
-        loads[3].wait()
-    left, right = [], []
+    left = []
     for m in range(block):
+        left.append([])
         for b in range(orb):
             plain = jnp.zeros((group_rows, lanes), f32)
             turned = plain
@@ -221,17 +246,22 @@
                 k_im = kw[m, c, b, 1:2, :]
                 plain += same[c] * k_re + turn[c] * k_im
                 turned += turn[c] * k_re - same[c] * k_im
-            for p, factor in enumerate((plain, turned)):
-                left.append(stacked(factor))
-                right.append(hist_ref[m, p, b].reshape(cols, lanes))
-    with jax.named_scope("VDOT"):
-        sums = dot(jnp.concatenate(left, axis=1), jnp.concatenate(right, axis=1), 1)
+            left[m] += [stacked(plain), stacked(turned)]
+    sums = jnp.zeros((2 * group_rows, cols), f32)
+    for m in range(block):
+        with jax.named_scope("LOADH"):
+            large[m].wait()
+        right = [hist_ref[m, p, b].reshape(cols, lanes) for b in range(orb) for p in range(2)]
+        sums += dot(jnp.concatenate(left[m], axis=1), jnp.concatenate(right, axis=1), 1)
+    with jax.named_scope("VSEND"):
         vsend[:, :cols] = folded(sums)
-    give(sum_copy)
+
+        give(direct_copy, direct)
+        give(sum_copy, me)
 
     with jax.named_scope("PC"):
-        for load in loads[4:]:
-            load.wait()
+        for copy in others:
+            copy.wait()
         half = group_rows * 2
         for m in range(block):
             h_re = pseudo_ref[m, 0].astype(f32)
@@ -248,7 +278,7 @@
         for t in range(n_hist):
             csend[t, :half, :] = hist_p[t * half : (t + 1) * half, :].astype(bf16)
             csend[t, half:, :] = tail
-    give(column_copy)
+    give(column_copy, me)
 
     def one_tile(tile, carry):
         at = pl.ds(pl.multiple_of(tile * tile_rows, tile_rows), tile_rows)
@@ -283,7 +313,7 @@
 
             @pl.when(target < me)
             def _():
-                part_copy(me, target).start()
+                part_copy(target).start()
 
         return carry
 
@@ -317,8 +347,20 @@
     later = jnp.where((step_col >= step_row) & (step_col < current), 1.0, 0.0).astype(bf16)
     inside = (row_of <= current) & (row_of >= first)
 
+    with jax.named_scope("WOPEN"):
+
+        @pl.when(me == 0)
+        def _():
+            pl.semaphore_wait(barrier, n_hist * n_ka - 1)
+
+            def one(target, carry):
+                signal(opened, target, my_ka)
+                return carry
+
+            lax.fori_loop(1, n_hist, one, 0)
+
     with jax.named_scope("TAKEE"):
-        take(energy_copy)
+        take(band_recv, got_energy)
     with jax.named_scope("FREE"):
         for t in range(n_hist):
             for c in range(orb):
@@ -347,14 +389,51 @@
         own = jnp.concatenate(pieces, axis=1) + vsend[...]
         own = jnp.where(lane_of == cols, count, own)
 
-    def take_sum(source, value):
-        sum_copy(source, me).wait_recv()
-        return value + vrecv[source]
+    xfree[...] = own
+    with jax.named_scope("WOPEN2"):
+
+        @pl.when(me > 0)
+        def _():
+            pl.semaphore_wait(opened, 1)
+
+    for hop in range(1, n_ka):
+        target = lax.rem(my_ka + hop, n_ka)
+
+        @pl.when((me < lead) & (target == 0))
+        def _():
+            local_copy(xfree, hop).start()
 
     with jax.named_scope("TAKEV"):
-        xsend[...] = lax.fori_loop(me + 1, n_hist, take_sum, own)
+
+        for t in range(n_hist - 1):
+            later_rows = pl.ds(t + 1, n_hist - 1 - t)
+
+            @pl.when((me == t) & is_root)
+            def _():
+                wait_bytes(vrecv.at[later_rows], got_sum)
+
+            @pl.when((me == t) & jnp.logical_not(is_root))
+            def _():
+                wait_bytes(vrecv.at[later_rows, my_ka], got_sum)
+
+    xsend[...] = lax.fori_loop(
+        me + 1, n_hist, lambda source, value: value + vrecv[source, my_ka], own
+    )
     for hop in range(1, n_ka):
-        local_copy(my_ka, lax.rem(my_ka + hop, n_ka)).start()
+        target = lax.rem(my_ka + hop, n_ka)
+
+        @pl.when((me >= lead) | (target != 0))
+        def _():
+            local_copy(xsend, hop).start()
+
+    @pl.when(is_root)
+    def _():
+        def one(source, value):
+            for ka in range(1, n_ka):
+                value = value + vrecv[source, ka]
+            return value
+
+        xfree[...] = lax.fori_loop(me + 1, n_hist, one, xsend[...])
 
     with jax.named_scope("TOTAL"):
         at = pl.ds(pl.multiple_of(first, block), block)
@@ -370,7 +449,7 @@
                 total_out[row : row + block, :] = d_re * f_im + d_im * f_re
 
     with jax.named_scope("TAKEC"):
-        take(column_copy)
+        take(crecv, got_column)
     with jax.named_scope("MIX"):
         for t in range(n_hist):
             hist_p[t * half : (t + 1) * half, :] = crecv[t, :half, :].astype(f32)
@@ -403,11 +482,10 @@
                 ).astype(bf16)
 
     with jax.named_scope("TAKEX"):
-        local = xsend[...]
+        wait_bytes(xrecv, got_local)
+        local = jnp.where(is_root, xfree[...], xsend[...])
         for hop in range(1, n_ka):
-            source = lax.rem(my_ka + hop, n_ka)
-            local_copy(source, my_ka).wait_recv()
-            local = local + xrecv[source]
+            local = local + xrecv[hop - 1]
     with jax.named_scope("FINAL"):
         scale = 1.0 / local[:, cols : cols + 1]
         picked = jnp.where(lane_of // times == lax.rem(group_of, orb), local, 0.0)
@@ -422,24 +500,32 @@
             )
         local_out[...] = pltpu.roll(local * scale, width - first, 1)
 
-    def take_part(source, value):
-        part_copy(source, me).wait_recv()
-        return value + precv[source].astype(f32)
-
     with jax.named_scope("TAKEP"):
-        fresh = total_out[...] + psend[me].astype(f32)
-        total_out[...] = lax.fori_loop(me + 1, n_hist, take_part, fresh)
-
-    def settle(target, carry):
-        energy_copy(me, target).wait_send()
-        sum_copy(me, target).wait_send()
-        column_copy(me, target).wait_send()
-        part_copy(me, target).wait_send()
-        return carry
-
-    lax.fori_loop(0, me, settle, 0)
-    for hop in range(1, n_ka):
-        local_copy(my_ka, lax.rem(my_ka + hop, n_ka)).wait_send()
+        take(precv, got_part)
+        total_out[...] = lax.fori_loop(
+            me + 1,
+            n_hist,
+            lambda source, value: value + precv[source].astype(f32),
+            total_out[...] + psend[me].astype(f32),
+        )
+
+    with jax.named_scope("SETTLE"):
+        for t in range(1, n_hist):
+
+            @pl.when(me == t)
+            def _():
+                wait_bytes(band_recv.at[pl.ds(0, t)], sent_energy)
+                wait_bytes(vrecv.at[pl.ds(0, t), 0], sent_sum)
+                wait_bytes(csend.at[pl.ds(0, t)], sent_column)
+                wait_bytes(psend.at[pl.ds(0, t)], sent_part)
+
+        for t in range(1, lead + 1):
+
+            @pl.when(direct == t)
+            def _():
+                wait_bytes(vrecv.at[pl.ds(0, t), 0], sent_direct)
+
+        wait_bytes(xrecv, sent_local)
 
 
 def lay_out(times, total_ref, local_ref, pseudo_ref, lattice_out, local_out, pseudo_out):
@@ -515,9 +601,10 @@
             pltpu.VMEM((orb, times, lanes), f32),
             pltpu.VMEM((2, orb, times, lanes), f32),
             pltpu.VMEM((group_rows, width), f32),
-            pltpu.VMEM((n_hist, group_rows, width), f32),
+            pltpu.VMEM((n_hist, n_ka, group_rows, width), f32),
             pltpu.VMEM((group_rows, width), f32),
-            pltpu.VMEM((n_ka, group_rows, width), f32),
+            pltpu.VMEM((group_rows, width), f32),
+            pltpu.VMEM((n_ka - 1, group_rows, width), f32),
             pltpu.VMEM((n_hist, rows, lanes), bf16),
             pltpu.VMEM((n_hist, rows, lanes), bf16),
             pltpu.VMEM((n_hist, 4 * group_rows, lanes), bf16),
@@ -527,10 +614,9 @@
             pltpu.VMEM((2 * states, 2 * orb * lanes), bf16),
             pltpu.VMEM((2 * width, 2 * block * states), bf16),
             pltpu.VMEM((per_tile, rows, lanes), f32),
-            dma((len(operands),)),
-            *[dma((n_hist,)) for _ in range(8)],
-            dma((n_ka,)),
-            dma((n_ka,)),
+            dma((len(operands) - 1 + block,)),
+            *[dma] * 11,
+            pltpu.SemaphoreType.REGULAR,
         ],
         compiler_params=pltpu.CompilerParams(collective_id=0, has_side_effects=True),
     )(

time: 16.5 us -> 14.7 us (0.89)
  Pallas kernels: 15 us -> 13.2 us
    pallas_call x1, Pallas kernels: 14.4 us -> 12.5 us  [per_device(): pl.pallas_call(functools.partial(kernel, n_hist, n_ka), out_shape=(pltpu....]
where the time goes in v3:
time: 14.7 us; the launch traced here: 14.5 us
  Pallas kernels  13.2 us (90%)
  between operations  1.29 us (9%)
    pallas_call x1, Pallas kernels, per_device(): pl.pallas_call(functools.partial(kernel, n_hist, n_ka), out_shape=(pltpu....  12.5 us
    pallas_call x1, Pallas kernels, per_device(): pl.pallas_call(functools.partial(lay_out, times), out_shape=(jax.ShapeDty...  0.68 us

profile of v3, /device:TPU:0, one launch (start us, length us, event | category | flops | bytes accessed | tf_op | source)
XLA Modules:
  0.0 14.5 jit_solution(1651383857768832472)
XLA Ops:
  1.3 12.5 %shard_map.121 = (f32[72,128]{1,0:T(8,128)S(1)}, f32[8,128]{1,0:T(8,128)S(1)}, f32[4,128]{1,0:T(4,128)S(1)}) custom-call(s32[1]{0:T(128)S(6)} %copy.13.step_ref, f32[3,4,128]{2,1,0:T(4,128)} %bitcast.14, bf16[4,3,3,2,128]{4,3,2,1,0:T(2,128)(2,1)} %bitcast.12, bf16[4,2,3,3,32,128]{5,4,3,2,1,0:T(8,128)(2,1)} %hist_any.1, f32[3,3,2,128]{3,2,1,0:T(2,128)} %bitcast.13, ...), custom_call_target="tpu_custom_call" | custom-call | tf_op jit(solution)/shard_map/pallas_call | solution.py:585
  13.8 0.7 %shard_map.122 = (bf16[4,3,3,2,128]{4,3,2,1,0:T(2,128)(2,1)}, f32[3,3,2,4]{3,2,1,0:T(2,128)}, f32[2,4,64]{2,1,0:T(4,128)}) custom-call(f32[72,128]{1,0:T(8,128)S(1)} %get-tuple-element.9.total_ref, f32[8,128]{1,0:T(8,128)S(1)} %get-tuple-element.10.local_ref, f32[4,128]{1,0:T(4,128)S(1)} %get-tuple-element.11.pseudo_ref), custom_call_target="tpu_custom_call" | custom-call | tf_op jit(solution)/shard_map/pallas_call | solution.py:626

commit v4 on v3

--- a/solution.py
+++ b/solution.py
@@ -36,6 +36,22 @@
 
 def folded(values):
     return values[:group_rows] + values[group_rows:]
+
+
+def minus_sine_cosine(angle):
+    quarter = jnp.floor(angle * 0.6366197723675814 + 0.5)
+    rest = angle - quarter * 1.5703125
+    rest = rest - quarter * 4.837512969970703125e-4
+    rest = rest - quarter * 7.54978995489188216e-8
+    square = rest * rest
+    sine = (-1.9515295891e-4 * square + 8.3321608736e-3) * square - 1.6666654611e-1
+    sine = sine * square * rest + rest
+    cosine = (2.443315711809948e-5 * square - 1.388731625493765e-3) * square
+    cosine = (cosine + 4.166664568298827e-2) * square * square - 0.5 * square + 1.0
+    half = jnp.floor(quarter * 0.5)
+    odd = quarter - 2.0 * half > 0.5
+    sign = 2.0 * (half - 2.0 * jnp.floor(half * 0.5)) - 1.0
+    return sign * jnp.where(odd, cosine, sine), sign * jnp.where(odd, -sine, cosine)
 
 
 def kernel(
@@ -51,7 +67,7 @@
     conn_any,
     pred_any,
     pseudo_any,
-    total_out,
+    lattice_out,
     local_out,
     pseudo_out,
     band_recv,
@@ -77,6 +93,9 @@
     precv,
     csend,
     crecv,
+    gsend,
+    grecv,
+    total,
     hist_p,
     hist_r,
     hits,
@@ -87,11 +106,14 @@
     sent_sum,
     sent_direct,
     sent_column,
+    sent_given,
     sent_part,
     sent_local,
     got_energy,
     got_sum,
+    got_direct,
     got_column,
+    got_given,
     got_part,
     got_local,
     opened,
@@ -172,13 +194,16 @@
         return remote(vsend, vrecv.at[me, my_ka], sent_sum, got_sum, target, my_ka)
 
     def direct_copy(target):
-        return remote(vsend, vrecv.at[me, my_ka], sent_direct, got_sum, target, 0)
+        return remote(vsend, vrecv.at[me, my_ka], sent_direct, got_direct, target, 0)
 
     def part_copy(target):
         return remote(psend.at[target], precv.at[me], sent_part, got_part, target, my_ka)
 
     def column_copy(target):
         return remote(csend.at[target], crecv.at[me], sent_column, got_column, target, my_ka)
+
+    def given_copy(target):
+        return remote(gsend, grecv.at[me], sent_given, got_given, target, my_ka)
 
     def local_copy(src, hop):
         target = lax.rem(my_ka + hop, n_ka)
@@ -262,7 +287,7 @@
     with jax.named_scope("PC"):
         for copy in others:
             copy.wait()
-        half = group_rows * 2
+        half = block * block
         for m in range(block):
             h_re = pseudo_ref[m, 0].astype(f32)
             h_im = pseudo_ref[m, 1].astype(f32)
@@ -271,14 +296,11 @@
                 hist_p[t * half + m * block : t * half + (m + 1) * block, :] = both[
                     t * block : (t + 1) * block
                 ]
-        given = jnp.concatenate([pred_ref[0], pred_ref[1]], axis=1)
-        tail = jnp.concatenate(
-            [*two_parts(given), jnp.zeros((half - 2 * block, lanes), f32)], axis=0
-        ).astype(bf16)
         for t in range(n_hist):
-            csend[t, :half, :] = hist_p[t * half : (t + 1) * half, :].astype(bf16)
-            csend[t, half:, :] = tail
+            csend[t] = hist_p[t * half : (t + 1) * half, :].astype(bf16)
+        gsend[...] = jnp.concatenate([pred_ref[0], pred_ref[1]], axis=1)
     give(column_copy, me)
+    give(given_copy, me)
 
     def one_tile(tile, carry):
         at = pl.ds(pl.multiple_of(tile * tile_rows, tile_rows), tile_rows)
@@ -321,6 +343,7 @@
         lax.fori_loop(0, first // tile_rows + 1, one_tile, 0)
 
     crecv[me] = csend[me]
+    grecv[me] = gsend[...]
     row_of = lax.broadcasted_iota(jnp.int32, (times, lanes), 0)
     lane_of = lax.broadcasted_iota(jnp.int32, (group_rows, width), 1)
     group_of = lax.broadcasted_iota(jnp.int32, (group_rows, width), 0)
@@ -339,7 +362,7 @@
     lane = lax.broadcasted_iota(jnp.int32, (block, 2 * states), 1)
     energies = jnp.concatenate([energy_ref[...], energy_ref[...]], axis=1)
     spins = energies * time_step * (current - line).astype(f32)
-    free_pseudo = jnp.where(lane < states, -jnp.sin(spins), -jnp.cos(spins))
+    free_pseudo = jnp.where(lane < states, *minus_sine_cosine(spins))
     free_pseudo = free_pseudo * jnp.where(line <= current, 1.0, 0.0)
     count = jnp.sum(mult, axis=1, keepdims=True)
     step_row = lax.broadcasted_iota(jnp.int32, (times, times), 0)
@@ -365,20 +388,23 @@
         for t in range(n_hist):
             for c in range(orb):
                 band_all[c, t * block : (t + 1) * block, :] = band_recv[t, c]
-        angle = jnp.zeros((times, orb * lanes), f32)
         rest = jnp.concatenate(
             [jnp.where(row_of >= first, band_all[c], 0.0) for c in range(orb)], axis=1
         )
+        bands = []
         for _ in range(3):
-            piece = rest.astype(bf16)
-            angle += dot(later, piece, 0)
-            rest = rest - piece.astype(f32)
+            bands.append(rest.astype(bf16))
+            rest = rest - bands[-1].astype(f32)
+        angle = dot(
+            jnp.concatenate([later] * 3, axis=1), jnp.concatenate(bands, axis=0), 0
+        )
         angle = angle * time_step
         pieces = []
         for c in range(orb):
             part = angle[:, c * lanes : (c + 1) * lanes]
-            free_re = jnp.where(inside, -jnp.sin(part), 0.0)
-            free_im = jnp.where(inside, -jnp.cos(part), 0.0)
+            free_re, free_im = minus_sine_cosine(part)
+            free_re = jnp.where(inside, free_re, 0.0)
+            free_im = jnp.where(inside, free_im, 0.0)
             free_all[0, c] = free_re
             free_all[1, c] = free_im
             two_re, two_im = two_parts(free_re), two_parts(free_im)
@@ -405,16 +431,7 @@
 
     with jax.named_scope("TAKEV"):
 
-        for t in range(n_hist - 1):
-            later_rows = pl.ds(t + 1, n_hist - 1 - t)
-
-            @pl.when((me == t) & is_root)
-            def _():
-                wait_bytes(vrecv.at[later_rows], got_sum)
-
-            @pl.when((me == t) & jnp.logical_not(is_root))
-            def _():
-                wait_bytes(vrecv.at[later_rows, my_ka], got_sum)
+        take(vrecv.at[:, my_ka], got_sum)
 
     xsend[...] = lax.fori_loop(
         me + 1, n_hist, lambda source, value: value + vrecv[source, my_ka], own
@@ -425,15 +442,6 @@
         @pl.when((me >= lead) | (target != 0))
         def _():
             local_copy(xsend, hop).start()
-
-    @pl.when(is_root)
-    def _():
-        def one(source, value):
-            for ka in range(1, n_ka):
-                value = value + vrecv[source, ka]
-            return value
-
-        xfree[...] = lax.fori_loop(me + 1, n_hist, one, xsend[...])
 
     with jax.named_scope("TOTAL"):
         at = pl.ds(pl.multiple_of(first, block), block)
@@ -444,21 +452,19 @@
                 d_re = dinv_ref[a, c, 0:1, :]
                 d_im = dinv_ref[a, c, 1:2, :]
                 row = (a * orb + c) * block
-                total_out[row : row + block, :] = d_re * f_re - d_im * f_im
+                total[row : row + block, :] = d_re * f_re - d_im * f_im
                 row += rows // 2
-                total_out[row : row + block, :] = d_re * f_im + d_im * f_re
+                total[row : row + block, :] = d_re * f_im + d_im * f_re
 
     with jax.named_scope("TAKEC"):
         take(crecv, got_column)
+        take(grecv, got_given)
     with jax.named_scope("MIX"):
         for t in range(n_hist):
-            hist_p[t * half : (t + 1) * half, :] = crecv[t, :half, :].astype(f32)
-            tail = crecv[t, half:, :].astype(f32)
-            for p in range(2):
-                at = p * times + t * block
-                hist_r[at : at + block, :] = tail[p * block : (p + 1) * block]
-        known = jnp.concatenate([row_of >= first] * 2, axis=0)
-        given = jnp.where(known, hist_r[...], 0.0).astype(bf16)
+            hist_p[t * half : (t + 1) * half, :] = crecv[t].astype(f32)
+            hist_r[t * block : (t + 1) * block, :] = grecv[t]
+        given = jnp.where(row_of >= first, hist_r[...], 0.0)
+        given = jnp.concatenate(two_parts(given), axis=0).astype(bf16)
         reached = dot(given, hits[...], 0)
         reached = reached[:times] + reached[times:]
         row_weight = jnp.where(row_of == 0, 0.5 * coupling, coupling)
@@ -481,6 +487,38 @@
                     r_re[a] * turned - r_im[a] * plain
                 ).astype(bf16)
 
+    with jax.named_scope("TAKEP"):
+        take(precv, got_part)
+        total[...] = lax.fori_loop(
+            me + 1,
+            n_hist,
+            lambda source, value: value + precv[source].astype(f32),
+            total[...] + psend[me].astype(f32),
+        )
+        for a in range(orb):
+            for c in range(orb):
+                for j in range(block):
+                    at = pl.ds((a * orb + c) * block + j, 2, stride=rows // 2)
+                    lattice_out[j, a, c] = total[at, :].astype(bf16)
+
+    with jax.named_scope("TAKED"):
+
+        @pl.when(is_root)
+        def _():
+            for t in range(min(lead, n_hist - 1)):
+
+                @pl.when(me == t)
+                def _():
+                    far = vrecv.at[pl.ds(t + 1, n_hist - 1 - t), pl.ds(1, n_ka - 1)]
+                    wait_bytes(far, got_direct)
+
+            def one(source, value):
+                for ka in range(1, n_ka):
+                    value = value + vrecv[source, ka]
+                return value
+
+            xfree[...] = lax.fori_loop(me + 1, n_hist, one, xsend[...])
+
     with jax.named_scope("TAKEX"):
         wait_bytes(xrecv, got_local)
         local = jnp.where(is_root, xfree[...], xsend[...])
@@ -495,19 +533,15 @@
         sums = folded(dot(stacked(picked), mix[...], 0))
         sums = jnp.sum(sums, axis=0, keepdims=True)
         for j in range(block):
-            pseudo_out[j : j + 1, :] = (
-                free_pseudo[j : j + 1] + sums[:, j * lanes : (j + 1) * lanes] * scale[:1]
-            )
-        local_out[...] = pltpu.roll(local * scale, width - first, 1)
-
-    with jax.named_scope("TAKEP"):
-        take(precv, got_part)
-        total_out[...] = lax.fori_loop(
-            me + 1,
-            n_hist,
-            lambda source, value: value + precv[source].astype(f32),
-            total_out[...] + psend[me].astype(f32),
-        )
+            row = free_pseudo[j : j + 1] + sums[:, j * lanes : (j + 1) * lanes] * scale[:1]
+            for p in range(2):
+                pseudo_out[p, j : j + 1, :] = row[:, p * states : (p + 1) * states]
+        local = local * scale
+        for c in range(orb):
+            own = pltpu.roll(local, width - first - c * times, 1)[:, :block]
+            for a in range(orb):
+                for p in range(2):
+                    local_out[a, c, p : p + 1, :] = own[p * orb + a : p * orb + a + 1]
 
     with jax.named_scope("SETTLE"):
         for t in range(1, n_hist):
@@ -517,6 +551,7 @@
                 wait_bytes(band_recv.at[pl.ds(0, t)], sent_energy)
                 wait_bytes(vrecv.at[pl.ds(0, t), 0], sent_sum)
                 wait_bytes(csend.at[pl.ds(0, t)], sent_column)
+                wait_bytes(grecv.at[pl.ds(0, t)], sent_given)
                 wait_bytes(psend.at[pl.ds(0, t)], sent_part)
 
         for t in range(1, lead + 1):
@@ -528,23 +563,16 @@
         wait_bytes(xrecv, sent_local)
 
 
-def lay_out(times, total_ref, local_ref, pseudo_ref, lattice_out, local_out, pseudo_out):
-    block, orb = lattice_out.shape[:2]
-    states = pseudo_out.shape[2]
-    half = total_ref.shape[0] // 2
-    for a in range(orb):
-        for c in range(orb):
-            row = (a * orb + c) * block
-            for j in range(block):
-                pair = total_ref[pl.ds(row + j, 2, stride=half), :]
-                lattice_out[j, a, c] = pair.astype(jnp.bfloat16)
-            for s in range(2):
-                row = s * orb + a
-                local_out[a, c, s : s + 1, :] = local_ref[
-                    row : row + 1, c * times : c * times + block
-                ]
-    for p in range(2):
-        pseudo_out[p] = pseudo_ref[:, p * states : (p + 1) * states]
+def put_out(*refs):
+    sources, targets, sems = refs[:3], refs[3:6], refs[6]
+    copies = [
+        pltpu.make_async_copy(source, target, sems.at[i])
+        for i, (source, target) in enumerate(zip(sources, targets))
+    ]
+    for copy in copies:
+        copy.start()
+    for copy in copies:
+        copy.wait()
 
 
 def per_device(
@@ -585,9 +613,9 @@
     results = pl.pallas_call(
         functools.partial(kernel, n_hist, n_ka),
         out_shape=(
-            pltpu.VMEM((rows, lanes), f32),
-            pltpu.VMEM((group_rows, width), f32),
-            pltpu.VMEM((block, 2 * states), f32),
+            pltpu.VMEM((block, orb, orb, 2, lanes), bf16),
+            pltpu.VMEM((orb, orb, 2, block), f32),
+            pltpu.VMEM((2, block, states), f32),
         ),
         in_specs=[pl.BlockSpec(memory_space=pltpu.SMEM)]
         + [pl.BlockSpec(memory_space=pl.ANY)] * len(operands),
@@ -607,15 +635,18 @@
             pltpu.VMEM((n_ka - 1, group_rows, width), f32),
             pltpu.VMEM((n_hist, rows, lanes), bf16),
             pltpu.VMEM((n_hist, rows, lanes), bf16),
-            pltpu.VMEM((n_hist, 4 * group_rows, lanes), bf16),
-            pltpu.VMEM((n_hist, 4 * group_rows, lanes), bf16),
+            pltpu.VMEM((n_hist, block * block, lanes), bf16),
+            pltpu.VMEM((n_hist, block * block, lanes), bf16),
+            pltpu.VMEM((block, 2 * states), f32),
+            pltpu.VMEM((n_hist, block, 2 * states), f32),
+            pltpu.VMEM((rows, lanes), f32),
             pltpu.VMEM((times * block, lanes), f32),
-            pltpu.VMEM((2 * times, lanes), f32),
+            pltpu.VMEM((times, lanes), f32),
             pltpu.VMEM((2 * states, 2 * orb * lanes), bf16),
             pltpu.VMEM((2 * width, 2 * block * states), bf16),
             pltpu.VMEM((per_tile, rows, lanes), f32),
             dma((len(operands) - 1 + block,)),
-            *[dma] * 11,
+            *[dma] * 14,
             pltpu.SemaphoreType.REGULAR,
         ],
         compiler_params=pltpu.CompilerParams(collective_id=0, has_side_effects=True),
@@ -624,14 +655,11 @@
         *operands,
     )
     lattice, local, pseudo = pl.pallas_call(
-        functools.partial(lay_out, times),
-        out_shape=(
-            jax.ShapeDtypeStruct((block, orb, orb, 2, lanes), bf16),
-            jax.ShapeDtypeStruct((orb, orb, 2, block), f32),
-            jax.ShapeDtypeStruct((2, block, states), f32),
-        ),
+        put_out,
+        out_shape=tuple(jax.ShapeDtypeStruct(array.shape, array.dtype) for array in results),
         in_specs=[vmem] * 3,
-        out_specs=(vmem, vmem, vmem),
+        out_specs=[pl.BlockSpec(memory_space=pl.ANY)] * 3,
+        scratch_shapes=[dma((3,))],
         compiler_params=pltpu.CompilerParams(vmem_limit_bytes=layout_bytes),
     )(*results)
     return (

time: 14.7 us -> 14.6 us (level)
  no operation moved by 1% of the time
where the time goes in v4:
time: 14.6 us; the launch traced here: 14.4 us
  Pallas kernels  13.1 us (90%)
  between operations  1.29 us (9%)
    pallas_call x1, Pallas kernels, per_device(): pl.pallas_call(functools.partial(kernel, n_hist, n_ka), out_shape=(pltpu....  12.5 us
    pallas_call x1, Pallas kernels, per_device(): pl.pallas_call(put_out, out_shape=tuple((jax.ShapeDtypeStruct(array.shape...  0.64 us

profile of v4, /device:TPU:0, one launch (start us, length us, event | category | flops | bytes accessed | tf_op | source)
XLA Modules:
  0.0 14.4 jit_solution(6604749860039886369)
XLA Ops:
  1.3 12.5 %shard_map.121 = (bf16[4,3,3,2,128]{4,3,2,1,0:T(2,128)(2,1)S(1)}, f32[3,3,2,4]{3,2,1,0:T(2,128)S(1)}, f32[2,4,64]{2,1,0:T(4,128)S(1)}) custom-call(s32[1]{0:T(128)S(6)} %copy.13.step_ref, f32[3,4,128]{2,1,0:T(4,128)} %bitcast.14, bf16[4,3,3,2,128]{4,3,2,1,0:T(2,128)(2,1)} %bitcast.12, bf16[4,2,3,3,32,128]{5,4,3,2,1,0:T(8,128)(2,1)} %hist_any.1, ...), custom_call_target="tpu_custom_call" | custom-call | tf_op jit(solution)/shard_map/pallas_call | solution.py:613
  13.8 0.6 %shard_map.122 = (bf16[4,3,3,2,128]{4,3,2,1,0:T(2,128)(2,1)}, f32[3,3,2,4]{3,2,1,0:T(2,128)}, f32[2,4,64]{2,1,0:T(4,128)}) custom-call(bf16[4,3,3,2,128]{4,3,2,1,0:T(2,128)(2,1)S(1)} %get-tuple-element.9.refs_0_, f32[3,3,2,4]{3,2,1,0:T(2,128)S(1)} %get-tuple-element.10.refs_1_, f32[2,4,64]{2,1,0:T(4,128)S(1)} %get-tuple-element.11.refs_2_), custom_call_target="tpu_custom_call" | custom-call | tf_op jit(solution)/shard_map/pallas_call | solution.py:657

commit v5 on v4

--- a/solution.py
+++ b/solution.py
@@ -80,14 +80,19 @@
     pred_ref,
     pseudo_ref,
     kw,
-    d_same,
-    d_turn,
+    d_both,
+    d_far,
+    band_far,
     band_all,
     free_all,
     vsend,
     vrecv,
+    wsend,
+    wrecv,
+    own_far,
     xsend,
     xfree,
+    xsum,
     xrecv,
     psend,
     precv,
@@ -105,6 +110,9 @@
     sent_energy,
     sent_sum,
     sent_direct,
+    sent_band,
+    sent_pack,
+    sent_own,
     sent_column,
     sent_given,
     sent_part,
@@ -112,6 +120,9 @@
     got_energy,
     got_sum,
     got_direct,
+    got_band,
+    got_pack,
+    got_own,
     got_column,
     got_given,
     got_part,
@@ -152,7 +163,7 @@
                 signal(barrier, target, ka)
             return carry
 
-        lax.fori_loop(me + 1, n_hist, one, 0)
+        lax.fori_loop(jnp.maximum(me, 1), n_hist, one, 0)
 
     for ka in range(n_ka):
 
@@ -194,7 +205,16 @@
         return remote(vsend, vrecv.at[me, my_ka], sent_sum, got_sum, target, my_ka)
 
     def direct_copy(target):
-        return remote(vsend, vrecv.at[me, my_ka], sent_direct, got_direct, target, 0)
+        return remote(wsend, wrecv.at[me, my_ka], sent_direct, got_direct, target, 0)
+
+    def band_copy(target):
+        return remote(band_any, band_far.at[me], sent_band, got_band, target, 0)
+
+    def pack_copy():
+        return remote(d_both, d_far, sent_pack, got_pack, me, 0)
+
+    def own_copy():
+        return remote(xfree, own_far, sent_own, got_own, me, 0)
 
     def part_copy(target):
         return remote(psend.at[target], precv.at[me], sent_part, got_part, target, my_ka)
@@ -209,12 +229,12 @@
         target = lax.rem(my_ka + hop, n_ka)
         return remote(src, xrecv.at[hop - 1], sent_local, got_local, me, target)
 
-    def give(copy, stop):
+    def give(copy, start, stop):
         def one(target, carry):
             copy(target).start()
             return carry
 
-        lax.fori_loop(0, stop, one, 0)
+        lax.fori_loop(start, stop, one, 0)
 
     def wait_bytes(ref, sem):
         pltpu.make_async_copy(ref, ref, sem).wait()
@@ -231,18 +251,24 @@
         jnp.where(first + m == 0, 0.5, 1.0) * jnp.where(first + m < current, 1.0, 0.0)
         for m in range(block)
     ]
-    d_same[...] = jnp.zeros(d_same.shape, f32)
-    d_turn[...] = jnp.zeros(d_turn.shape, f32)
+    d_both[...] = jnp.zeros(d_both.shape, f32)
     vsend[...] = jnp.zeros(vsend.shape, f32)
-
-    direct = jnp.where(my_ka == 0, 0, jnp.minimum(me, lead))
+    wsend[...] = jnp.zeros(wsend.shape, bf16)
+
+    near = jnp.minimum(me, lead)
+    direct = jnp.where(my_ka == 0, 0, near)
+    beside_root = (my_ka != 0) & (me < lead)
+    is_far = my_ka == n_ka - 1
+    banded = jnp.where(is_far, near, 0)
+    early = jnp.where(my_ka == 0, near, 0)
     with jax.named_scope("WBAR"):
 
         @pl.when(me > 0)
         def _():
-            pl.semaphore_wait(barrier, me + direct)
-
-    give(energy_copy, me)
+            pl.semaphore_wait(barrier, me + direct + jnp.where(beside_root, 1, 0))
+
+    give(band_copy, 0, banded)
+    give(energy_copy, 0, me)
 
     with jax.named_scope("LOAD"):
         for copy in small:
@@ -254,12 +280,12 @@
         for c in range(orb):
             d_re = dinv_ref[a, c, 0:1, :] * mult
             d_im = dinv_ref[a, c, 1:2, :] * mult
-            d_same[c, a : a + 1, :] = d_re
-            d_same[c, orb + a : orb + a + 1, :] = d_im
-            d_turn[c, a : a + 1, :] = -d_im
-            d_turn[c, orb + a : orb + a + 1, :] = d_re
-    same = [d_same[c] for c in range(orb)]
-    turn = [d_turn[c] for c in range(orb)]
+            d_both[0, c, a : a + 1, :] = d_re
+            d_both[0, c, orb + a : orb + a + 1, :] = d_im
+            d_both[1, c, a : a + 1, :] = -d_im
+            d_both[1, c, orb + a : orb + a + 1, :] = d_re
+    same = [d_both[0, c] for c in range(orb)]
+    turn = [d_both[1, c] for c in range(orb)]
     left = []
     for m in range(block):
         left.append([])
@@ -279,10 +305,11 @@
         right = [hist_ref[m, p, b].reshape(cols, lanes) for b in range(orb) for p in range(2)]
         sums += dot(jnp.concatenate(left[m], axis=1), jnp.concatenate(right, axis=1), 1)
     with jax.named_scope("VSEND"):
-        vsend[:, :cols] = folded(sums)
-
-        give(direct_copy, direct)
-        give(sum_copy, me)
+        sums = folded(sums)
+        vsend[:, :cols] = sums
+        wsend[:, :cols] = sums.astype(bf16)
+        give(direct_copy, 0, direct)
+        give(sum_copy, 0, me)
 
     with jax.named_scope("PC"):
         for copy in others:
@@ -299,8 +326,8 @@
         for t in range(n_hist):
             csend[t] = hist_p[t * half : (t + 1) * half, :].astype(bf16)
         gsend[...] = jnp.concatenate([pred_ref[0], pred_ref[1]], axis=1)
-    give(column_copy, me)
-    give(given_copy, me)
+    give(column_copy, 0, near)
+    give(given_copy, 0, near)
 
     def one_tile(tile, carry):
         at = pl.ds(pl.multiple_of(tile * tile_rows, tile_rows), tile_rows)
@@ -333,7 +360,7 @@
             target = tile * per_tile + d
             psend[target] = stage[d].astype(bf16)
 
-            @pl.when(target < me)
+            @pl.when(target < early)
             def _():
                 part_copy(target).start()
 
@@ -365,67 +392,75 @@
     free_pseudo = jnp.where(lane < states, *minus_sine_cosine(spins))
     free_pseudo = free_pseudo * jnp.where(line <= current, 1.0, 0.0)
     count = jnp.sum(mult, axis=1, keepdims=True)
-    step_row = lax.broadcasted_iota(jnp.int32, (times, times), 0)
-    step_col = lax.broadcasted_iota(jnp.int32, (times, times), 1)
-    later = jnp.where((step_col >= step_row) & (step_col < current), 1.0, 0.0).astype(bf16)
     inside = (row_of <= current) & (row_of >= first)
-
-    with jax.named_scope("WOPEN"):
-
-        @pl.when(me == 0)
-        def _():
-            pl.semaphore_wait(barrier, n_hist * n_ka - 1)
-
-            def one(target, carry):
-                signal(opened, target, my_ka)
-                return carry
-
-            lax.fori_loop(1, n_hist, one, 0)
-
-    with jax.named_scope("TAKEE"):
-        take(band_recv, got_energy)
-    with jax.named_scope("FREE"):
+    summed = (row_of < current) & (row_of >= first)
+
+    def free_sums(bands, place, same, turn, keep):
         for t in range(n_hist):
             for c in range(orb):
-                band_all[c, t * block : (t + 1) * block, :] = band_recv[t, c]
-        rest = jnp.concatenate(
-            [jnp.where(row_of >= first, band_all[c], 0.0) for c in range(orb)], axis=1
-        )
-        bands = []
-        for _ in range(3):
-            bands.append(rest.astype(bf16))
-            rest = rest - bands[-1].astype(f32)
-        angle = dot(
-            jnp.concatenate([later] * 3, axis=1), jnp.concatenate(bands, axis=0), 0
-        )
-        angle = angle * time_step
+                band_all[place, c, t * block : (t + 1) * block, :] = bands[t, c]
         pieces = []
         for c in range(orb):
-            part = angle[:, c * lanes : (c + 1) * lanes]
-            free_re, free_im = minus_sine_cosine(part)
+            angle = jnp.where(summed, band_all[place, c] * time_step, 0.0)
+            shift = 1
+            while shift < times:
+                after = jnp.zeros((shift, lanes), f32)
+                angle = angle + jnp.concatenate([angle[shift:], after], axis=0)
+                shift *= 2
+            free_re, free_im = minus_sine_cosine(angle)
             free_re = jnp.where(inside, free_re, 0.0)
             free_im = jnp.where(inside, free_im, 0.0)
-            free_all[0, c] = free_re
-            free_all[1, c] = free_im
+            if keep:
+                free_all[0, c] = free_re
+                free_all[1, c] = free_im
             two_re, two_im = two_parts(free_re), two_parts(free_im)
             right = jnp.concatenate([two_re[0], two_im[0], two_re[1], two_im[1]], axis=1)
             left = jnp.concatenate([stacked(same[c]), stacked(turn[c])] * 2, axis=1)
             pieces.append(folded(dot(left, right.astype(bf16), 1)))
         pieces.append(jnp.zeros((group_rows, width - cols), f32))
-        own = jnp.concatenate(pieces, axis=1) + vsend[...]
+        return jnp.concatenate(pieces, axis=1)
+
+    with jax.named_scope("WOPEN"):
+
+        @pl.when(me == 0)
+        def _():
+            pl.semaphore_wait(barrier, n_hist * n_ka - 1)
+
+            def one(target, carry):
+                signal(opened, target, my_ka)
+                return carry
+
+            lax.fori_loop(1, n_hist, one, 0)
+
+    @pl.when(beside_root & is_far)
+    def _():
+        xfree[...] = jnp.where(lane_of == cols, count, vsend[...])
+        band_copy(me).start()
+        pack_copy().start()
+        own_copy().start()
+
+    with jax.named_scope("TAKEE"):
+        take(band_recv, got_energy)
+    with jax.named_scope("FREE"):
+        own = free_sums(band_recv, 0, same, turn, True) + vsend[...]
         own = jnp.where(lane_of == cols, count, own)
-
-    xfree[...] = own
+    give(column_copy, near, me)
+    give(given_copy, near, me)
+    give(part_copy, early, me)
     with jax.named_scope("WOPEN2"):
 
         @pl.when(me > 0)
         def _():
             pl.semaphore_wait(opened, 1)
+
+    @pl.when(beside_root & jnp.logical_not(is_far))
+    def _():
+        xfree[...] = own
 
     for hop in range(1, n_ka):
         target = lax.rem(my_ka + hop, n_ka)
 
-        @pl.when((me < lead) & (target == 0))
+        @pl.when(beside_root & jnp.logical_not(is_far) & (target == 0))
         def _():
             local_copy(xfree, hop).start()
 
@@ -442,6 +477,23 @@
         @pl.when((me >= lead) | (target != 0))
         def _():
             local_copy(xsend, hop).start()
+
+    with jax.named_scope("TAKEB"):
+
+        @pl.when(is_root)
+        def _():
+            for t in range(lead):
+
+                @pl.when(me == t)
+                def _():
+                    wait_bytes(band_far.at[pl.ds(t, n_hist - t)], got_band)
+
+            wait_bytes(d_far, got_pack)
+            wait_bytes(own_far, got_own)
+            same_far = [d_far[0, c] for c in range(orb)]
+            turn_far = [d_far[1, c] for c in range(orb)]
+            value = free_sums(band_far, 1, same_far, turn_far, False)
+            xsum[...] = value + xsend[...] + own_far[...]
 
     with jax.named_scope("TOTAL"):
         at = pl.ds(pl.multiple_of(first, block), block)
@@ -487,6 +539,24 @@
                     r_re[a] * turned - r_im[a] * plain
                 ).astype(bf16)
 
+    with jax.named_scope("TAKED"):
+
+        @pl.when(is_root)
+        def _():
+            for t in range(min(lead, n_hist - 1)):
+
+                @pl.when(me == t)
+                def _():
+                    above, beside = pl.ds(t + 1, n_hist - 1 - t), pl.ds(1, n_ka - 1)
+                    wait_bytes(wrecv.at[above, beside], got_direct)
+
+            def one(source, value):
+                for ka in range(1, n_ka):
+                    value = value + wrecv[source, ka].astype(f32)
+                return value
+
+            xsum[...] = lax.fori_loop(me + 1, n_hist, one, xsum[...])
+
     with jax.named_scope("TAKEP"):
         take(precv, got_part)
         total[...] = lax.fori_loop(
@@ -501,29 +571,25 @@
                     at = pl.ds((a * orb + c) * block + j, 2, stride=rows // 2)
                     lattice_out[j, a, c] = total[at, :].astype(bf16)
 
-    with jax.named_scope("TAKED"):
+    with jax.named_scope("TAKEX"):
+
+        @pl.when(jnp.logical_not(is_root))
+        def _():
+            wait_bytes(xrecv, got_local)
+            value = xsend[...]
+            for hop in range(1, n_ka):
+                value += xrecv[hop - 1]
+            xsum[...] = value
 
         @pl.when(is_root)
         def _():
-            for t in range(min(lead, n_hist - 1)):
-
-                @pl.when(me == t)
-                def _():
-                    far = vrecv.at[pl.ds(t + 1, n_hist - 1 - t), pl.ds(1, n_ka - 1)]
-                    wait_bytes(far, got_direct)
-
-            def one(source, value):
-                for ka in range(1, n_ka):
-                    value = value + vrecv[source, ka]
-                return value
-
-            xfree[...] = lax.fori_loop(me + 1, n_hist, one, xsend[...])
-
-    with jax.named_scope("TAKEX"):
-        wait_bytes(xrecv, got_local)
-        local = jnp.where(is_root, xfree[...], xsend[...])
-        for hop in range(1, n_ka):
-            local = local + xrecv[hop - 1]
+            wait_bytes(xrecv.at[pl.ds(1, n_ka - 2)], got_local)
+            value = xsum[...]
+            for hop in range(2, n_ka):
+                value += xrecv[hop - 1]
+            xsum[...] = value
+
+        local = xsum[...]
     with jax.named_scope("FINAL"):
         scale = 1.0 / local[:, cols : cols + 1]
         picked = jnp.where(lane_of // times == lax.rem(group_of, orb), local, 0.0)
@@ -558,9 +624,21 @@
 
             @pl.when(direct == t)
             def _():
-                wait_bytes(vrecv.at[pl.ds(0, t), 0], sent_direct)
-
-        wait_bytes(xrecv, sent_local)
+                wait_bytes(wrecv.at[pl.ds(0, t), 0], sent_direct)
+
+            @pl.when(banded + jnp.where(beside_root & is_far, 1, 0) == t)
+            def _():
+                wait_bytes(band_far.at[pl.ds(0, t)], sent_band)
+
+        @pl.when(beside_root & is_far)
+        def _():
+            wait_bytes(d_both, sent_pack)
+            wait_bytes(xfree, sent_own)
+            wait_bytes(xrecv.at[pl.ds(0, n_ka - 2)], sent_local)
+
+        @pl.when(jnp.logical_not(beside_root & is_far))
+        def _():
+            wait_bytes(xrecv, sent_local)
 
 
 def put_out(*refs):
@@ -624,12 +702,17 @@
             pltpu.VMEM((n_hist, *operands[0].shape), f32),
             *[pltpu.VMEM(array.shape, array.dtype) for array in operands[1:]],
             pltpu.VMEM((block, orb, orb, 2, lanes), f32),
-            pltpu.VMEM((orb, group_rows, lanes), f32),
-            pltpu.VMEM((orb, group_rows, lanes), f32),
-            pltpu.VMEM((orb, times, lanes), f32),
+            pltpu.VMEM((2, orb, group_rows, lanes), f32),
+            pltpu.VMEM((2, orb, group_rows, lanes), f32),
+            pltpu.VMEM((n_hist, *operands[0].shape), f32),
+            pltpu.VMEM((2, orb, times, lanes), f32),
             pltpu.VMEM((2, orb, times, lanes), f32),
             pltpu.VMEM((group_rows, width), f32),
             pltpu.VMEM((n_hist, n_ka, group_rows, width), f32),
+            pltpu.VMEM((group_rows, width), bf16),
+            pltpu.VMEM((n_hist, n_ka, group_rows, width), bf16),
+            pltpu.VMEM((group_rows, width), f32),
+            pltpu.VMEM((group_rows, width), f32),
             pltpu.VMEM((group_rows, width), f32),
             pltpu.VMEM((group_rows, width), f32),
             pltpu.VMEM((n_ka - 1, group_rows, width), f32),
@@ -646,7 +729,7 @@
             pltpu.VMEM((2 * width, 2 * block * states), bf16),
             pltpu.VMEM((per_tile, rows, lanes), f32),
             dma((len(operands) - 1 + block,)),
-            *[dma] * 14,
+            *[dma] * 20,
             pltpu.SemaphoreType.REGULAR,
         ],
         compiler_params=pltpu.CompilerParams(collective_id=0, has_side_effects=True),

time: 14.6 us -> 13.5 us (0.925)
  Pallas kernels: 13.1 us -> 12 us
    pallas_call x1, Pallas kernels: 12.5 us -> 11.4 us  [per_device(): pl.pallas_call(functools.partial(kernel, n_hist, n_ka), out_shape=(pltpu....]
where the time goes in v5:
time: 13.5 us; the launch traced here: 13.3 us
  Pallas kernels  12 us (89%)
  between operations  1.29 us (10%)
    pallas_call x1, Pallas kernels, per_device(): pl.pallas_call(functools.partial(kernel, n_hist, n_ka), out_shape=(pltpu....  11.4 us
    pallas_call x1, Pallas kernels, per_device(): pl.pallas_call(put_out, out_shape=tuple((jax.ShapeDtypeStruct(array.shape...  0.64 us

profile of v5, /device:TPU:0, one launch (start us, length us, event | category | flops | bytes accessed | tf_op | source)
XLA Modules:
  0.0 13.3 jit_solution(7265970301730937357)
XLA Ops:
  1.3 11.4 %shard_map.121 = (bf16[4,3,3,2,128]{4,3,2,1,0:T(2,128)(2,1)S(1)}, f32[3,3,2,4]{3,2,1,0:T(2,128)S(1)}, f32[2,4,64]{2,1,0:T(4,128)S(1)}) custom-call(s32[1]{0:T(128)S(6)} %copy.13.step_ref, f32[3,4,128]{2,1,0:T(4,128)} %bitcast.14, bf16[4,3,3,2,128]{4,3,2,1,0:T(2,128)(2,1)} %bitcast.12, bf16[4,2,3,3,32,128]{5,4,3,2,1,0:T(8,128)(2,1)} %hist_any.1, ...), custom_call_target="tpu_custom_call" | custom-call | tf_op jit(solution)/shard_map/pallas_call | solution.py:691
  12.7 0.6 %shard_map.122 = (bf16[4,3,3,2,128]{4,3,2,1,0:T(2,128)(2,1)}, f32[3,3,2,4]{3,2,1,0:T(2,128)}, f32[2,4,64]{2,1,0:T(4,128)}) custom-call(bf16[4,3,3,2,128]{4,3,2,1,0:T(2,128)(2,1)S(1)} %get-tuple-element.9.refs_0_, f32[3,3,2,4]{3,2,1,0:T(2,128)S(1)} %get-tuple-element.10.refs_1_, f32[2,4,64]{2,1,0:T(4,128)S(1)} %get-tuple-element.11.refs_2_), custom_call_target="tpu_custom_call" | custom-call | tf_op jit(solution)/shard_map/pallas_call | solution.py:740

commit v6 on v5

--- a/solution.py
+++ b/solution.py
@@ -1,4 +1,5 @@
 import functools
+import math
 
 import jax
 import jax.numpy as jnp
@@ -13,6 +14,7 @@
 group_rows = 8
 lead = 2
 lane_count = 128
+unit_bytes = 4 * lane_count
 layout_bytes = 4 * 1024 * 1024
 
 
@@ -23,6 +25,12 @@
 
 def stacked(values):
     return jnp.concatenate(two_parts(values), axis=0).astype(jnp.bfloat16)
+
+
+def size_of(ref):
+    size = math.prod(ref.shape) * jnp.dtype(ref.dtype).itemsize
+    assert size % unit_bytes == 0
+    return size // unit_bytes
 
 
 def dot(left, right, contract):
@@ -95,6 +103,8 @@
     xsum,
     xrecv,
     psend,
+    pair_recv,
+    paired,
     precv,
     csend,
     crecv,
@@ -106,28 +116,19 @@
     hits,
     mix,
     stage,
+    units,
     load_sem,
-    sent_energy,
-    sent_sum,
-    sent_direct,
-    sent_band,
-    sent_pack,
-    sent_own,
-    sent_column,
-    sent_given,
-    sent_part,
-    sent_local,
+    sent,
     got_energy,
     got_sum,
     got_direct,
-    got_band,
-    got_pack,
-    got_own,
+    got_far,
     got_column,
-    got_given,
+    got_pair,
     got_part,
     got_local,
     opened,
+    root_in,
 ):
     _, orb, block, lanes = band_recv.shape
     times = hist_ref.shape[4]
@@ -141,6 +142,9 @@
     me = lax.axis_index("hist")
     my_ka = lax.axis_index("ka")
     first = me * block
+    parity = lax.rem(me, 2)
+    chip = (me - parity) // 2
+    partner = me + 1 - 2 * parity
 
     barrier = pltpu.get_barrier_semaphore()
 
@@ -165,6 +169,10 @@
 
         lax.fori_loop(jnp.maximum(me, 1), n_hist, one, 0)
 
+    @pl.when((parity == 1) & (me > 1))
+    def _():
+        signal(barrier, partner, my_ka)
+
     for ka in range(n_ka):
 
         @pl.when((me > 0) | (my_ka != ka))
@@ -176,17 +184,26 @@
         copy.start()
         return copy
 
-    pairs_in = [(krow_any, krow_ref), (dinv_any, dinv_ref), (mult_any, mult_ref)]
-    pairs_in += [(hist_any.at[m], hist_ref.at[m]) for m in range(block)]
-    pairs_in += [
-        (pred_any, pred_ref),
-        (pseudo_any, pseudo_ref),
-        (energy_any, energy_ref),
-        (conn_any, conn_ref),
+    small = [
+        (krow_any, krow_ref), (dinv_any, dinv_ref), (mult_any, mult_ref),
         (band_any, band_recv.at[me]),
     ]
-    loads = [load(source, target, i) for i, (source, target) in enumerate(pairs_in)]
-    small, large, others = loads[:3], loads[3 : 3 + block], loads[3 + block :]
+    for source, target in small:
+        load(source, target, 0)
+    large = [load(hist_any.at[m], hist_ref.at[m], 1 + m) for m in range(block)]
+    others = [
+        load(source, target, 1 + block + i)
+        for i, (source, target) in enumerate(
+            (
+                (pred_any, pred_ref),
+                (pseudo_any, pseudo_ref),
+                (energy_any, energy_ref),
+                (conn_any, conn_ref),
+            )
+        )
+    ]
+    is_far = my_ka == n_ka - 1
+    far_class = jnp.where(is_far, 1, 0)
 
     def remote(src, dst, send_sem, recv_sem, hist, ka):
         return pltpu.make_async_remote_copy(
@@ -199,35 +216,43 @@
         )
 
     def energy_copy(target):
-        return remote(band_any, band_recv.at[me], sent_energy, got_energy, target, my_ka)
+        return remote(band_any, band_recv.at[me], sent, got_energy, target, my_ka)
 
     def sum_copy(target):
-        return remote(vsend, vrecv.at[me, my_ka], sent_sum, got_sum, target, my_ka)
+        return remote(vsend, vrecv.at[me, my_ka], sent, got_sum, target, my_ka)
 
     def direct_copy(target):
-        return remote(wsend, wrecv.at[me, my_ka], sent_direct, got_direct, target, 0)
+        return remote(wsend, wrecv.at[me, my_ka], sent, got_direct, target, 0)
 
     def band_copy(target):
-        return remote(band_any, band_far.at[me], sent_band, got_band, target, 0)
+        return remote(band_any, band_far.at[my_ka, me], sent, got_far.at[far_class], target, 0)
 
     def pack_copy():
-        return remote(d_both, d_far, sent_pack, got_pack, me, 0)
+        return remote(d_both.at[0], d_far.at[my_ka], sent, got_far.at[far_class], me, 0)
 
     def own_copy():
-        return remote(xfree, own_far, sent_own, got_own, me, 0)
-
-    def part_copy(target):
-        return remote(psend.at[target], precv.at[me], sent_part, got_part, target, my_ka)
+        return remote(xfree, own_far.at[my_ka], sent, got_far.at[far_class], me, 0)
+
+    def pair_copy(place):
+        source = psend.at[2 * place + 1 - parity]
+        return remote(source, pair_recv.at[place], sent, got_pair, partner, my_ka)
+
+    def part_copy(place):
+        target = 2 * place + parity
+        return remote(paired.at[place], precv.at[me], sent, got_part, target, my_ka)
+
+    def beside_copy():
+        return remote(psend.at[partner], precv.at[me], sent, got_part, partner, my_ka)
 
     def column_copy(target):
-        return remote(csend.at[target], crecv.at[me], sent_column, got_column, target, my_ka)
+        return remote(csend.at[target], crecv.at[me], sent, got_column, target, my_ka)
 
     def given_copy(target):
-        return remote(gsend, grecv.at[me], sent_given, got_given, target, my_ka)
+        return remote(gsend, grecv.at[me], sent, got_column, target, my_ka)
 
     def local_copy(src, hop):
         target = lax.rem(my_ka + hop, n_ka)
-        return remote(src, xrecv.at[hop - 1], sent_local, got_local, me, target)
+        return remote(src, xrecv.at[hop - 1], sent, got_local, me, target)
 
     def give(copy, start, stop):
         def one(target, carry):
@@ -238,6 +263,13 @@
 
     def wait_bytes(ref, sem):
         pltpu.make_async_copy(ref, ref, sem).wait()
+
+    def wait_units(count, sem):
+        wait_bytes(units.at[pl.ds(0, count)], sem)
+
+    e_size, v_size, w_size = size_of(band_any), size_of(vsend), size_of(wsend)
+    c_size, p_size = size_of(csend.at[0]) + size_of(gsend), size_of(psend.at[0])
+    pack_size = size_of(d_far.at[0]) + size_of(own_far.at[0])
 
     def take(ref, sem):
         for t in range(n_hist - 1):
@@ -258,22 +290,30 @@
     near = jnp.minimum(me, lead)
     direct = jnp.where(my_ka == 0, 0, near)
     beside_root = (my_ka != 0) & (me < lead)
-    is_far = my_ka == n_ka - 1
-    banded = jnp.where(is_far, near, 0)
-    early = jnp.where(my_ka == 0, near, 0)
+    packs = (my_ka != 0) & ((me == 0) | ((me < lead) & is_far))
+    shares = beside_root & jnp.logical_not(packs)
+    banded = jnp.where(is_far, near, jnp.where(my_ka == 0, 0, jnp.minimum(me, 1)))
+    early = jnp.minimum(chip, lead // 2)
     with jax.named_scope("WBAR"):
 
         @pl.when(me > 0)
         def _():
-            pl.semaphore_wait(barrier, me + direct + jnp.where(beside_root, 1, 0))
+            others_in = jnp.where(beside_root, 1, 0) + jnp.where(parity == 0, 1, 0)
+            pl.semaphore_wait(barrier, me + direct + others_in)
 
     give(band_copy, 0, banded)
     give(energy_copy, 0, me)
 
+    @pl.when((me == 1) & (my_ka != 0))
+    def _():
+        signal(root_in, 0, my_ka)
+
+
     with jax.named_scope("LOAD"):
-        for copy in small:
-            copy.wait()
+        wait_units(sum(size_of(source) for source, _ in small), load_sem.at[0])
     mult = mult_ref[...].astype(f32)
+    count = jnp.sum(mult, axis=1, keepdims=True)
+    lane_of = lax.broadcasted_iota(jnp.int32, (group_rows, width), 1)
     for m in range(block):
         kw[m] = krow_ref[m].astype(f32) * weight[m]
     for a in range(orb):
@@ -311,6 +351,17 @@
         give(direct_copy, 0, direct)
         give(sum_copy, 0, me)
 
+    @pl.when(packs)
+    def _():
+        @pl.when(me == 0)
+        def _():
+            pl.semaphore_wait(root_in, 1)
+
+        xfree[...] = jnp.where(lane_of == cols, count, vsend[...])
+        band_copy(me).start()
+        own_copy().start()
+        pack_copy().start()
+
     with jax.named_scope("PC"):
         for copy in others:
             copy.wait()
@@ -360,9 +411,13 @@
             target = tile * per_tile + d
             psend[target] = stage[d].astype(bf16)
 
-            @pl.when(target < early)
+            @pl.when((target < 2 * chip) & (parity != d % 2))
             def _():
-                part_copy(target).start()
+                pair_copy(tile * (per_tile // 2) + d // 2).start()
+
+            @pl.when((target == partner) & (parity == 1))
+            def _():
+                beside_copy().start()
 
         return carry
 
@@ -372,7 +427,6 @@
     crecv[me] = csend[me]
     grecv[me] = gsend[...]
     row_of = lax.broadcasted_iota(jnp.int32, (times, lanes), 0)
-    lane_of = lax.broadcasted_iota(jnp.int32, (group_rows, width), 1)
     group_of = lax.broadcasted_iota(jnp.int32, (group_rows, width), 0)
     conn = jnp.concatenate([conn_ref[...], conn_ref[...]], axis=1)
     reach = lax.broadcasted_iota(jnp.int32, (2 * states, 2 * states), 0)
@@ -391,7 +445,6 @@
     spins = energies * time_step * (current - line).astype(f32)
     free_pseudo = jnp.where(lane < states, *minus_sine_cosine(spins))
     free_pseudo = free_pseudo * jnp.where(line <= current, 1.0, 0.0)
-    count = jnp.sum(mult, axis=1, keepdims=True)
     inside = (row_of <= current) & (row_of >= first)
     summed = (row_of < current) & (row_of >= first)
 
@@ -420,6 +473,21 @@
         pieces.append(jnp.zeros((group_rows, width - cols), f32))
         return jnp.concatenate(pieces, axis=1)
 
+    with jax.named_scope("PAIR"):
+        for n in range(1, n_hist // 2):
+
+            @pl.when(chip == n)
+            def _():
+                wait_bytes(pair_recv.at[pl.ds(0, n)], got_pair)
+
+        def combine(place, carry):
+            value = psend[2 * place + parity].astype(f32) + pair_recv[place].astype(f32)
+            paired[place] = value.astype(bf16)
+            return carry
+
+        lax.fori_loop(0, chip, combine, 0)
+    give(part_copy, 0, early)
+
     with jax.named_scope("WOPEN"):
 
         @pl.when(me == 0)
@@ -431,13 +499,6 @@
                 return carry
 
             lax.fori_loop(1, n_hist, one, 0)
-
-    @pl.when(beside_root & is_far)
-    def _():
-        xfree[...] = jnp.where(lane_of == cols, count, vsend[...])
-        band_copy(me).start()
-        pack_copy().start()
-        own_copy().start()
 
     with jax.named_scope("TAKEE"):
         take(band_recv, got_energy)
@@ -446,21 +507,21 @@
         own = jnp.where(lane_of == cols, count, own)
     give(column_copy, near, me)
     give(given_copy, near, me)
-    give(part_copy, early, me)
+    give(part_copy, early, chip)
     with jax.named_scope("WOPEN2"):
 
         @pl.when(me > 0)
         def _():
             pl.semaphore_wait(opened, 1)
 
-    @pl.when(beside_root & jnp.logical_not(is_far))
+    @pl.when(shares)
     def _():
         xfree[...] = own
 
     for hop in range(1, n_ka):
         target = lax.rem(my_ka + hop, n_ka)
 
-        @pl.when(beside_root & jnp.logical_not(is_far) & (target == 0))
+        @pl.when(shares & (target == 0))
         def _():
             local_copy(xfree, hop).start()
 
@@ -477,23 +538,6 @@
         @pl.when((me >= lead) | (target != 0))
         def _():
             local_copy(xsend, hop).start()
-
-    with jax.named_scope("TAKEB"):
-
-        @pl.when(is_root)
-        def _():
-            for t in range(lead):
-
-                @pl.when(me == t)
-                def _():
-                    wait_bytes(band_far.at[pl.ds(t, n_hist - t)], got_band)
-
-            wait_bytes(d_far, got_pack)
-            wait_bytes(own_far, got_own)
-            same_far = [d_far[0, c] for c in range(orb)]
-            turn_far = [d_far[1, c] for c in range(orb)]
-            value = free_sums(band_far, 1, same_far, turn_far, False)
-            xsum[...] = value + xsend[...] + own_far[...]
 
     with jax.named_scope("TOTAL"):
         at = pl.ds(pl.multiple_of(first, block), block)
@@ -509,8 +553,12 @@
                 total[row : row + block, :] = d_re * f_im + d_im * f_re
 
     with jax.named_scope("TAKEC"):
-        take(crecv, got_column)
-        take(grecv, got_given)
+        for t in range(n_hist - 1):
+
+            @pl.when(me == t)
+            def _():
+                wait_units((n_hist - 1 - t) * c_size, got_column)
+
     with jax.named_scope("MIX"):
         for t in range(n_hist):
             hist_p[t * half : (t + 1) * half, :] = crecv[t].astype(f32)
@@ -539,6 +587,39 @@
                     r_re[a] * turned - r_im[a] * plain
                 ).astype(bf16)
 
+    def far_sums(ka):
+        same_far = [d_far[ka, c] for c in range(orb)]
+        turn_far = [
+            jnp.concatenate(
+                [-far[orb : 2 * orb], far[:orb], jnp.zeros((group_rows - 2 * orb, lanes), f32)],
+                axis=0,
+            )
+            for far in same_far
+        ]
+        return free_sums(band_far.at[ka], ka, same_far, turn_far, False) + own_far[ka]
+
+    with jax.named_scope("TAKEB"):
+
+        @pl.when(is_root & (me == 0))
+        def _():
+            line_size = n_hist * e_size + pack_size
+            wait_units((n_ka - 2) * line_size, got_far.at[0])
+            value = xsend[...]
+            for ka in range(1, n_ka - 1):
+                value += far_sums(ka)
+            wait_units(line_size, got_far.at[1])
+            xsum[...] = value + far_sums(n_ka - 1)
+
+        @pl.when(is_root & (me > 0))
+        def _():
+            for t in range(1, lead):
+
+                @pl.when(me == t)
+                def _():
+                    wait_units((n_hist - t) * e_size + pack_size, got_far.at[1])
+
+            xsum[...] = xsend[...] + far_sums(n_ka - 1)
+
     with jax.named_scope("TAKED"):
 
         @pl.when(is_root)
@@ -558,13 +639,24 @@
             xsum[...] = lax.fori_loop(me + 1, n_hist, one, xsum[...])
 
     with jax.named_scope("TAKEP"):
-        take(precv, got_part)
+        for t in range(n_hist - 1):
+            above = n_hist // 2 - 1 - t // 2 + (1 - t % 2)
+
+            @pl.when(me == t)
+            def _():
+                wait_bytes(precv.at[pl.ds(0, above)], got_part)
+
         total[...] = lax.fori_loop(
-            me + 1,
-            n_hist,
-            lambda source, value: value + precv[source].astype(f32),
+            chip + 1,
+            n_hist // 2,
+            lambda place, value: value + precv[2 * place + parity].astype(f32),
             total[...] + psend[me].astype(f32),
         )
+
+        @pl.when(parity == 0)
+        def _():
+            total[...] += precv[partner].astype(f32)
+
         for a in range(orb):
             for c in range(orb):
                 for j in range(block):
@@ -581,7 +673,7 @@
                 value += xrecv[hop - 1]
             xsum[...] = value
 
-        @pl.when(is_root)
+        @pl.when(is_root & (me > 0))
         def _():
             wait_bytes(xrecv.at[pl.ds(1, n_ka - 2)], got_local)
             value = xsum[...]
@@ -610,35 +702,24 @@
                     local_out[a, c, p : p + 1, :] = own[p * orb + a : p * orb + a + 1]
 
     with jax.named_scope("SETTLE"):
-        for t in range(1, n_hist):
-
-            @pl.when(me == t)
-            def _():
-                wait_bytes(band_recv.at[pl.ds(0, t)], sent_energy)
-                wait_bytes(vrecv.at[pl.ds(0, t), 0], sent_sum)
-                wait_bytes(csend.at[pl.ds(0, t)], sent_column)
-                wait_bytes(grecv.at[pl.ds(0, t)], sent_given)
-                wait_bytes(psend.at[pl.ds(0, t)], sent_part)
-
-        for t in range(1, lead + 1):
-
-            @pl.when(direct == t)
-            def _():
-                wait_bytes(wrecv.at[pl.ds(0, t), 0], sent_direct)
-
-            @pl.when(banded + jnp.where(beside_root & is_far, 1, 0) == t)
-            def _():
-                wait_bytes(band_far.at[pl.ds(0, t)], sent_band)
-
-        @pl.when(beside_root & is_far)
-        def _():
-            wait_bytes(d_both, sent_pack)
-            wait_bytes(xfree, sent_own)
-            wait_bytes(xrecv.at[pl.ds(0, n_ka - 2)], sent_local)
-
-        @pl.when(jnp.logical_not(beside_root & is_far))
-        def _():
-            wait_bytes(xrecv, sent_local)
+        for t in range(n_hist):
+            line = t * (e_size + v_size + c_size) + (2 * (t // 2) + t % 2) * p_size
+            leads = min(t, lead)
+            for kind in range(3):
+                if kind == 0:
+                    at, bands, packed, directs = my_ka == 0, 0, 0, 0
+                elif kind == 1:
+                    at = (my_ka > 0) & (my_ka < n_ka - 1)
+                    bands, packed, directs = 1, int(t == 0), leads
+                else:
+                    at, packed, directs = is_far, int(t < lead), leads
+                    bands = leads + packed
+                size = line + directs * w_size + bands * e_size + packed * pack_size
+                size += (n_ka - 1 - packed) * v_size
+
+                @pl.when((me == t) & at)
+                def _():
+                    wait_units(size, sent)
 
 
 def put_out(*refs):
@@ -674,6 +755,13 @@
     rows = pairs * block
     per_tile = tile_rows // block
     width = -(-(orb * times + 1) // lane_count) * lane_count
+    band_bytes = 4 * orb * block * lanes
+    tile_bytes = 4 * group_rows * width
+    most = n_hist * (
+        band_bytes + tile_bytes + (2 * block + 8) * block * lanes + 2 * rows * lanes
+    )
+    most += (n_ka + lead + n_hist) * tile_bytes + n_ka * n_hist * band_bytes
+    most //= unit_bytes
     vmem = pl.BlockSpec(memory_space=pltpu.VMEM)
     f32, bf16 = jnp.float32, jnp.bfloat16
     dma = pltpu.SemaphoreType.DMA
@@ -703,20 +791,22 @@
             *[pltpu.VMEM(array.shape, array.dtype) for array in operands[1:]],
             pltpu.VMEM((block, orb, orb, 2, lanes), f32),
             pltpu.VMEM((2, orb, group_rows, lanes), f32),
-            pltpu.VMEM((2, orb, group_rows, lanes), f32),
-            pltpu.VMEM((n_hist, *operands[0].shape), f32),
-            pltpu.VMEM((2, orb, times, lanes), f32),
+            pltpu.VMEM((n_ka, orb, group_rows, lanes), f32),
+            pltpu.VMEM((n_ka, n_hist, *operands[0].shape), f32),
+            pltpu.VMEM((n_ka, orb, times, lanes), f32),
             pltpu.VMEM((2, orb, times, lanes), f32),
             pltpu.VMEM((group_rows, width), f32),
             pltpu.VMEM((n_hist, n_ka, group_rows, width), f32),
             pltpu.VMEM((group_rows, width), bf16),
             pltpu.VMEM((n_hist, n_ka, group_rows, width), bf16),
-            pltpu.VMEM((group_rows, width), f32),
+            pltpu.VMEM((n_ka, group_rows, width), f32),
             pltpu.VMEM((group_rows, width), f32),
             pltpu.VMEM((group_rows, width), f32),
             pltpu.VMEM((group_rows, width), f32),
             pltpu.VMEM((n_ka - 1, group_rows, width), f32),
             pltpu.VMEM((n_hist, rows, lanes), bf16),
+            pltpu.VMEM((n_hist // 2, rows, lanes), bf16),
+            pltpu.VMEM((n_hist // 2, rows, lanes), bf16),
             pltpu.VMEM((n_hist, rows, lanes), bf16),
             pltpu.VMEM((n_hist, block * block, lanes), bf16),
             pltpu.VMEM((n_hist, block * block, lanes), bf16),
@@ -728,8 +818,12 @@
             pltpu.VMEM((2 * states, 2 * orb * lanes), bf16),
             pltpu.VMEM((2 * width, 2 * block * states), bf16),
             pltpu.VMEM((per_tile, rows, lanes), f32),
-            dma((len(operands) - 1 + block,)),
-            *[dma] * 20,
+            pltpu.VMEM((most, 1, lane_count), f32),
+            dma((block + 5,)),
+            *[dma] * 4,
+            dma((2,)),
+            *[dma] * 4,
+            pltpu.SemaphoreType.REGULAR,
             pltpu.SemaphoreType.REGULAR,
         ],
         compiler_params=pltpu.CompilerParams(collective_id=0, has_side_effects=True),

time: 13.5 us -> 12.9 us (0.956)
  Pallas kernels: 12 us -> 11.4 us
    pallas_call x1, Pallas kernels: 11.4 us -> 10.8 us  [per_device(): pl.pallas_call(functools.partial(kernel, n_hist, n_ka), out_shape=(pltpu....]
where the time goes in v6:
time: 12.9 us; the launch traced here: 12.7 us
  Pallas kernels  11.4 us (88%)
  between operations  1.29 us (10%)
    pallas_call x1, Pallas kernels, per_device(): pl.pallas_call(functools.partial(kernel, n_hist, n_ka), out_shape=(pltpu....  10.8 us
    pallas_call x1, Pallas kernels, per_device(): pl.pallas_call(put_out, out_shape=tuple((jax.ShapeDtypeStruct(array.shape...  0.64 us

profile of v6, /device:TPU:0, one launch (start us, length us, event | category | flops | bytes accessed | tf_op | source)
XLA Modules:
  0.0 12.7 jit_solution(394625935871153293)
XLA Ops:
  1.3 10.8 %shard_map.121 = (bf16[4,3,3,2,128]{4,3,2,1,0:T(2,128)(2,1)S(1)}, f32[3,3,2,4]{3,2,1,0:T(2,128)S(1)}, f32[2,4,64]{2,1,0:T(4,128)S(1)}) custom-call(s32[1]{0:T(128)S(6)} %copy.13.step_ref, f32[3,4,128]{2,1,0:T(4,128)} %bitcast.14, bf16[4,3,3,2,128]{4,3,2,1,0:T(2,128)(2,1)} %bitcast.12, bf16[4,2,3,3,32,128]{5,4,3,2,1,0:T(8,128)(2,1)} %hist_any.1, ...), custom_call_target="tpu_custom_call" | custom-call | tf_op jit(solution)/shard_map/pallas_call | solution.py:779
  12.0 0.6 %shard_map.122 = (bf16[4,3,3,2,128]{4,3,2,1,0:T(2,128)(2,1)}, f32[3,3,2,4]{3,2,1,0:T(2,128)}, f32[2,4,64]{2,1,0:T(4,128)}) custom-call(bf16[4,3,3,2,128]{4,3,2,1,0:T(2,128)(2,1)S(1)} %get-tuple-element.9.refs_0_, f32[3,3,2,4]{3,2,1,0:T(2,128)S(1)} %get-tuple-element.10.refs_1_, f32[2,4,64]{2,1,0:T(4,128)S(1)} %get-tuple-element.11.refs_2_), custom_call_target="tpu_custom_call" | custom-call | tf_op jit(solution)/shard_map/pallas_call | solution.py:834

commit v7 on v6

--- a/solution.py
+++ b/solution.py
@@ -146,39 +146,6 @@
     chip = (me - parity) // 2
     partner = me + 1 - 2 * parity
 
-    barrier = pltpu.get_barrier_semaphore()
-
-    def signal(sem, hist, ka):
-        pl.semaphore_signal(
-            sem, inc=1, device_id={"hist": hist, "ka": ka}, device_id_type=pl.DeviceIdType.MESH
-        )
-
-    def greet(target, carry):
-        signal(barrier, target, my_ka)
-        return carry
-
-    lax.fori_loop(me + 1, n_hist, greet, 0)
-    is_root = (my_ka == 0) & (me < lead)
-
-    @pl.when(is_root)
-    def _():
-        def one(target, carry):
-            for ka in range(1, n_ka):
-                signal(barrier, target, ka)
-            return carry
-
-        lax.fori_loop(jnp.maximum(me, 1), n_hist, one, 0)
-
-    @pl.when((parity == 1) & (me > 1))
-    def _():
-        signal(barrier, partner, my_ka)
-
-    for ka in range(n_ka):
-
-        @pl.when((me > 0) | (my_ka != ka))
-        def _():
-            signal(barrier, 0, ka)
-
     def load(source, target, place):
         copy = pltpu.make_async_copy(source, target, load_sem.at[place])
         copy.start()
@@ -202,6 +169,39 @@
             )
         )
     ]
+    barrier = pltpu.get_barrier_semaphore()
+
+    def signal(sem, hist, ka):
+        pl.semaphore_signal(
+            sem, inc=1, device_id={"hist": hist, "ka": ka}, device_id_type=pl.DeviceIdType.MESH
+        )
+
+    def greet(target, carry):
+        signal(barrier, target, my_ka)
+        return carry
+
+    lax.fori_loop(me + 1, n_hist, greet, 0)
+    is_root = (my_ka == 0) & (me < lead)
+
+    @pl.when(is_root)
+    def _():
+        def one(target, carry):
+            for ka in range(1, n_ka):
+                signal(barrier, target, ka)
+            return carry
+
+        lax.fori_loop(jnp.maximum(me, 1), n_hist, one, 0)
+
+    @pl.when((parity == 1) & (me > 1))
+    def _():
+        signal(barrier, partner, my_ka)
+
+    for ka in range(n_ka):
+
+        @pl.when((me > 0) | (my_ka != ka))
+        def _():
+            signal(barrier, 0, ka)
+
     is_far = my_ka == n_ka - 1
     far_class = jnp.where(is_far, 1, 0)
 
@@ -343,7 +343,8 @@
         with jax.named_scope("LOADH"):
             large[m].wait()
         right = [hist_ref[m, p, b].reshape(cols, lanes) for b in range(orb) for p in range(2)]
-        sums += dot(jnp.concatenate(left[m], axis=1), jnp.concatenate(right, axis=1), 1)
+        for x in range(orb):
+            sums += dot(jnp.concatenate(left[m][2*x:2*x+2], axis=1), jnp.concatenate(right[2*x:2*x+2], axis=1), 1)
     with jax.named_scope("VSEND"):
         sums = folded(sums)
         vsend[:, :cols] = sums

time: 12.9 us -> 12.9 us (level)
  no operation moved by 1% of the time
where the time goes in v7:
time: 12.9 us; the launch traced here: 12.7 us
  Pallas kernels  11.4 us (88%)
  between operations  1.29 us (10%)
    pallas_call x1, Pallas kernels, per_device(): pl.pallas_call(functools.partial(kernel, n_hist, n_ka), out_shape=(pltpu....  10.7 us
    pallas_call x1, Pallas kernels, per_device(): pl.pallas_call(put_out, out_shape=tuple((jax.ShapeDtypeStruct(array.shape...  0.64 us

profile of v7, /device:TPU:0, one launch (start us, length us, event | category | flops | bytes accessed | tf_op | source)
XLA Modules:
  0.0 12.7 jit_solution(14184444168532163644)
XLA Ops:
  1.3 10.7 %shard_map.121 = (bf16[4,3,3,2,128]{4,3,2,1,0:T(2,128)(2,1)S(1)}, f32[3,3,2,4]{3,2,1,0:T(2,128)S(1)}, f32[2,4,64]{2,1,0:T(4,128)S(1)}) custom-call(s32[1]{0:T(128)S(6)} %copy.13.step_ref, f32[3,4,128]{2,1,0:T(4,128)} %bitcast.14, bf16[4,3,3,2,128]{4,3,2,1,0:T(2,128)(2,1)} %bitcast.12, bf16[4,2,3,3,32,128]{5,4,3,2,1,0:T(8,128)(2,1)} %hist_any.1, ...), custom_call_target="tpu_custom_call" | custom-call | tf_op jit(solution)/shard_map/pallas_call | solution.py:780
  12.0 0.6 %shard_map.122 = (bf16[4,3,3,2,128]{4,3,2,1,0:T(2,128)(2,1)}, f32[3,3,2,4]{3,2,1,0:T(2,128)}, f32[2,4,64]{2,1,0:T(4,128)}) custom-call(bf16[4,3,3,2,128]{4,3,2,1,0:T(2,128)(2,1)S(1)} %get-tuple-element.9.refs_0_, f32[3,3,2,4]{3,2,1,0:T(2,128)S(1)} %get-tuple-element.10.refs_1_, f32[2,4,64]{2,1,0:T(4,128)S(1)} %get-tuple-element.11.refs_2_), custom_call_target="tpu_custom_call" | custom-call | tf_op jit(solution)/shard_map/pallas_call | solution.py:835

commit v8 on v7

--- a/solution.py
+++ b/solution.py
@@ -350,7 +350,10 @@
         vsend[:, :cols] = sums
         wsend[:, :cols] = sums.astype(bf16)
         give(direct_copy, 0, direct)
-        give(sum_copy, 0, me)
+        next_chip = jnp.minimum(me, lead + 1)
+        give(sum_copy, near, next_chip)
+        give(sum_copy, 0, near)
+        give(sum_copy, next_chip, me)
 
     @pl.when(packs)
     def _():
@@ -621,23 +624,25 @@
 
             xsum[...] = xsend[...] + far_sums(n_ka - 1)
 
-    with jax.named_scope("TAKED"):
-
-        @pl.when(is_root)
-        def _():
-            for t in range(min(lead, n_hist - 1)):
-
-                @pl.when(me == t)
+    with jax.named_scope("SETTLE"):
+        for t in range(n_hist):
+            line = t * (e_size + v_size + c_size) + (2 * (t // 2) + t % 2) * p_size
+            leads = min(t, lead)
+            for kind in range(3):
+                if kind == 0:
+                    at, bands, packed, directs = my_ka == 0, 0, 0, 0
+                elif kind == 1:
+                    at = (my_ka > 0) & (my_ka < n_ka - 1)
+                    bands, packed, directs = 1, int(t == 0), leads
+                else:
+                    at, packed, directs = is_far, int(t < lead), leads
+                    bands = leads + packed
+                size = line + directs * w_size + bands * e_size + packed * pack_size
+                size += (n_ka - 1 - packed) * v_size
+
+                @pl.when((me == t) & at)
                 def _():
-                    above, beside = pl.ds(t + 1, n_hist - 1 - t), pl.ds(1, n_ka - 1)
-                    wait_bytes(wrecv.at[above, beside], got_direct)
-
-            def one(source, value):
-                for ka in range(1, n_ka):
-                    value = value + wrecv[source, ka].astype(f32)
-                return value
-
-            xsum[...] = lax.fori_loop(me + 1, n_hist, one, xsum[...])
+                    wait_units(size, sent)
 
     with jax.named_scope("TAKEP"):
         for t in range(n_hist - 1):
@@ -663,6 +668,24 @@
                 for j in range(block):
                     at = pl.ds((a * orb + c) * block + j, 2, stride=rows // 2)
                     lattice_out[j, a, c] = total[at, :].astype(bf16)
+
+    with jax.named_scope("TAKED"):
+
+        @pl.when(is_root)
+        def _():
+            for t in range(min(lead, n_hist - 1)):
+
+                @pl.when(me == t)
+                def _():
+                    above, beside = pl.ds(t + 1, n_hist - 1 - t), pl.ds(1, n_ka - 1)
+                    wait_bytes(wrecv.at[above, beside], got_direct)
+
+            def one(source, value):
+                for ka in range(1, n_ka):
+                    value = value + wrecv[source, ka].astype(f32)
+                return value
+
+            xsum[...] = lax.fori_loop(me + 1, n_hist, one, xsum[...])
 
     with jax.named_scope("TAKEX"):
 
@@ -701,26 +724,6 @@
             for a in range(orb):
                 for p in range(2):
                     local_out[a, c, p : p + 1, :] = own[p * orb + a : p * orb + a + 1]
-
-    with jax.named_scope("SETTLE"):
-        for t in range(n_hist):
-            line = t * (e_size + v_size + c_size) + (2 * (t // 2) + t % 2) * p_size
-            leads = min(t, lead)
-            for kind in range(3):
-                if kind == 0:
-                    at, bands, packed, directs = my_ka == 0, 0, 0, 0
-                elif kind == 1:
-                    at = (my_ka > 0) & (my_ka < n_ka - 1)
-                    bands, packed, directs = 1, int(t == 0), leads
-                else:
-                    at, packed, directs = is_far, int(t < lead), leads
-                    bands = leads + packed
-                size = line + directs * w_size + bands * e_size + packed * pack_size
-                size += (n_ka - 1 - packed) * v_size
-
-                @pl.when((me == t) & at)
-                def _():
-                    wait_units(size, sent)
 
 
 def put_out(*refs):

time: 12.9 us -> 12.7 us (0.984)
  no operation moved by 1% of the time
where the time goes in v8:
time: 12.7 us; the launch traced here: 12.6 us
  Pallas kernels  11.3 us (89%)
  between operations  1.29 us (10%)
    pallas_call x1, Pallas kernels, per_device(): pl.pallas_call(functools.partial(kernel, n_hist, n_ka), out_shape=(pltpu....  10.6 us
    pallas_call x1, Pallas kernels, per_device(): pl.pallas_call(put_out, out_shape=tuple((jax.ShapeDtypeStruct(array.shape...  0.64 us

profile of v8, /device:TPU:0, one launch (start us, length us, event | category | flops | bytes accessed | tf_op | source)
XLA Modules:
  0.0 12.6 jit_solution(16645554293453937650)
XLA Ops:
  1.3 10.6 %shard_map.121 = (bf16[4,3,3,2,128]{4,3,2,1,0:T(2,128)(2,1)S(1)}, f32[3,3,2,4]{3,2,1,0:T(2,128)S(1)}, f32[2,4,64]{2,1,0:T(4,128)S(1)}) custom-call(s32[1]{0:T(128)S(6)} %copy.13.step_ref, f32[3,4,128]{2,1,0:T(4,128)} %bitcast.14, bf16[4,3,3,2,128]{4,3,2,1,0:T(2,128)(2,1)} %bitcast.12, bf16[4,2,3,3,32,128]{5,4,3,2,1,0:T(8,128)(2,1)} %hist_any.1, ...), custom_call_target="tpu_custom_call" | custom-call | tf_op jit(solution)/shard_map/pallas_call | solution.py:783
  11.9 0.6 %shard_map.122 = (bf16[4,3,3,2,128]{4,3,2,1,0:T(2,128)(2,1)}, f32[3,3,2,4]{3,2,1,0:T(2,128)}, f32[2,4,64]{2,1,0:T(4,128)}) custom-call(bf16[4,3,3,2,128]{4,3,2,1,0:T(2,128)(2,1)S(1)} %get-tuple-element.9.refs_0_, f32[3,3,2,4]{3,2,1,0:T(2,128)S(1)} %get-tuple-element.10.refs_1_, f32[2,4,64]{2,1,0:T(4,128)S(1)} %get-tuple-element.11.refs_2_), custom_call_target="tpu_custom_call" | custom-call | tf_op jit(solution)/shard_map/pallas_call | solution.py:838

commit v9 on v8

--- a/solution.py
+++ b/solution.py
@@ -326,9 +326,8 @@
             d_both[1, c, orb + a : orb + a + 1, :] = d_re
     same = [d_both[0, c] for c in range(orb)]
     turn = [d_both[1, c] for c in range(orb)]
-    left = []
-    for m in range(block):
-        left.append([])
+    def factors(m):
+        found = []
         for b in range(orb):
             plain = jnp.zeros((group_rows, lanes), f32)
             turned = plain
@@ -337,14 +336,19 @@
                 k_im = kw[m, c, b, 1:2, :]
                 plain += same[c] * k_re + turn[c] * k_im
                 turned += turn[c] * k_re - same[c] * k_im
-            left[m] += [stacked(plain), stacked(turned)]
+            found.append(jnp.concatenate([stacked(plain), stacked(turned)], axis=1))
+        return found
+
     sums = jnp.zeros((2 * group_rows, cols), f32)
+    left = factors(0)
     for m in range(block):
         with jax.named_scope("LOADH"):
             large[m].wait()
-        right = [hist_ref[m, p, b].reshape(cols, lanes) for b in range(orb) for p in range(2)]
-        for x in range(orb):
-            sums += dot(jnp.concatenate(left[m][2*x:2*x+2], axis=1), jnp.concatenate(right[2*x:2*x+2], axis=1), 1)
+        for b in range(orb):
+            right = [hist_ref[m, p, b].reshape(cols, lanes) for p in range(2)]
+            sums += dot(left[b], jnp.concatenate(right, axis=1), 1)
+        if m + 1 < block:
+            left = factors(m + 1)
     with jax.named_scope("VSEND"):
         sums = folded(sums)
         vsend[:, :cols] = sums

time: 12.7 us -> 12.8 us (level)
  no operation moved by 1% of the time
where the time goes in v9:
time: 12.8 us; the launch traced here: 12.6 us
  Pallas kernels  11.3 us (88%)
  between operations  1.29 us (10%)
    pallas_call x1, Pallas kernels, per_device(): pl.pallas_call(functools.partial(kernel, n_hist, n_ka), out_shape=(pltpu....  10.6 us
    pallas_call x1, Pallas kernels, per_device(): pl.pallas_call(put_out, out_shape=tuple((jax.ShapeDtypeStruct(array.shape...  0.64 us

profile of v9, /device:TPU:0, one launch (start us, length us, event | category | flops | bytes accessed | tf_op | source)
XLA Modules:
  0.0 12.6 jit_solution(11592497340458950276)
XLA Ops:
  1.3 10.6 %shard_map.121 = (bf16[4,3,3,2,128]{4,3,2,1,0:T(2,128)(2,1)S(1)}, f32[3,3,2,4]{3,2,1,0:T(2,128)S(1)}, f32[2,4,64]{2,1,0:T(4,128)S(1)}) custom-call(s32[1]{0:T(128)S(6)} %copy.13.step_ref, f32[3,4,128]{2,1,0:T(4,128)} %bitcast.14, bf16[4,3,3,2,128]{4,3,2,1,0:T(2,128)(2,1)} %bitcast.12, bf16[4,2,3,3,32,128]{5,4,3,2,1,0:T(8,128)(2,1)} %hist_any.1, ...), custom_call_target="tpu_custom_call" | custom-call | tf_op jit(solution)/shard_map/pallas_call | solution.py:787
  11.9 0.6 %shard_map.122 = (bf16[4,3,3,2,128]{4,3,2,1,0:T(2,128)(2,1)}, f32[3,3,2,4]{3,2,1,0:T(2,128)}, f32[2,4,64]{2,1,0:T(4,128)}) custom-call(bf16[4,3,3,2,128]{4,3,2,1,0:T(2,128)(2,1)S(1)} %get-tuple-element.9.refs_0_, f32[3,3,2,4]{3,2,1,0:T(2,128)S(1)} %get-tuple-element.10.refs_1_, f32[2,4,64]{2,1,0:T(4,128)S(1)} %get-tuple-element.11.refs_2_), custom_call_target="tpu_custom_call" | custom-call | tf_op jit(solution)/shard_map/pallas_call | solution.py:842
